TPU v7x, 32 devices: a whole 2x2x4 slice. The times are simulated.
32 devices in a mesh: seq: 4 (over x, core), fsdp: 8 (over z, y).
Axes of the slice: x: 2, y: 2, z: 4, core: 2. Of those that a mesh axis runs over, the one named last changes fastest.
Arguments:
- hidden_in: bfloat16 [8, 1024, 2048], P('fsdp', 'seq'), may hold values from -6 to 6
- out_cotangent: bfloat16 [8, 1024, 2048], P('fsdp', 'seq'), may hold values from -6 to 6
- seg_ids: int32 [8, 1024], P('fsdp'), may hold values from 0 to 2, as said below
- mixer_master: float32 [2048, 2304], P(('seq', 'fsdp')), may hold values from -0.125 to 0.125
- mixer_first: float32 [2048, 2304], P(('seq', 'fsdp')), may hold values from -0.6 to 0.6
- mixer_second: float32 [2048, 2304], P(('seq', 'fsdp')), may hold values from 0.01 to 0.1
- project_master: float32 [2048, 2048], P(('seq', 'fsdp')), may hold values from -1 to 1
- project_first: float32 [2048, 2048], P(('seq', 'fsdp')), may hold values from -0.6 to 0.6
- project_second: float32 [2048, 2048], P(('seq', 'fsdp')), may hold values from 0.01 to 0.1
- expand_master: float32 [2048, 8192], P(('seq', 'fsdp')), may hold values from -0.125 to 0.125
- expand_first: float32 [2048, 8192], P(('seq', 'fsdp')), may hold values from -0.6 to 0.6
- expand_second: float32 [2048, 8192], P(('seq', 'fsdp')), may hold values from 0.01 to 0.1
- reduce_master: float32 [8192, 2048], P(('seq', 'fsdp')), may hold values from -0.0625 to 0.0625
- reduce_first: float32 [8192, 2048], P(('seq', 'fsdp')), may hold values from -0.6 to 0.6
- reduce_second: float32 [8192, 2048], P(('seq', 'fsdp')), may hold values from 0.01 to 0.1
- affine_master: float32 [4, 2048], replicated
- affine_first: float32 [4, 2048], replicated, may hold values from -0.6 to 0.6
- affine_second: float32 [4, 2048], replicated, may hold values from 0.1 to 20
Outputs:
- block_output: bfloat16 [8, 1024, 2048], P('fsdp', 'seq')
- input_grad: bfloat16 [8, 1024, 2048], P('fsdp', 'seq')
- grad_norm: float32 [], replicated
- mixer_updated: float32 [2048, 2304], P(('seq', 'fsdp'))
- mixer_first_new: float32 [2048, 2304], P(('seq', 'fsdp'))
- mixer_second_new: float32 [2048, 2304], P(('seq', 'fsdp'))
- project_updated: float32 [2048, 2048], P(('seq', 'fsdp'))
- project_first_new: float32 [2048, 2048], P(('seq', 'fsdp'))
- project_second_new: float32 [2048, 2048], P(('seq', 'fsdp'))
- expand_updated: float32 [2048, 8192], P(('seq', 'fsdp'))
- expand_first_new: float32 [2048, 8192], P(('seq', 'fsdp'))
- expand_second_new: float32 [2048, 8192], P(('seq', 'fsdp'))
- reduce_updated: float32 [8192, 2048], P(('seq', 'fsdp'))
- reduce_first_new: float32 [8192, 2048], P(('seq', 'fsdp'))
- reduce_second_new: float32 [8192, 2048], P(('seq', 'fsdp'))
- affine_step: float32 [4, 2048], replicated
- affine_first_new: float32 [4, 2048], replicated
- affine_second_new: float32 [4, 2048], replicated
Inputs may be any that keep to these rules, and one draw needn't show every extreme that they name: `seg_ids`: in each group the prompt holds 512 tokens with id 0 and each of the 2 continuations (ids 1 to 2) holds 256 tokens; every segment is one contiguous run, in an order drawn for each group.
All inputs are finite; a program needn't handle non-finite values.
Results may differ from a plain program's by a relative error of at most 0.014.
Values may be sent and summed in bfloat16 or wider, within the bound.
No kernel may reach another device: no remote copies, remote signals or barrier semaphores. Data moves between devices by JAX's collectives and lax.ppermute only.
A program may use at most 576 MiB of HBM per device.

v0:
```python
import functools
import math

import jax
import jax.numpy as jnp
from jax import lax
from jax.experimental import pallas as pl
from jax.experimental.pallas import tpu as pltpu
from jax.sharding import PartitionSpec as P


D = 2048
FF = 8192
HEADS = 16
HEAD = 128
STEP = 10
KV = 2 * HEAD

norm_epsilon = 1e-05
adam_epsilon = 1e-08
first_decay = 0.9
second_decay = 0.95
learn_rate = 0.03
decay_rate = 0.1
masked_score = -1e30
low = jnp.bfloat16


def layer_norm(values_in, norm_gain, norm_shift):
    centered = values_in - jnp.mean(values_in, axis=-1, keepdims=True)
    variance = jnp.mean(centered * centered, axis=-1, keepdims=True)
    return centered * lax.rsqrt(variance + norm_epsilon) * norm_gain + norm_shift


def activate(pre_act):
    return jax.nn.gelu(pre_act, approximate=True)


def product(left_side, right_side):
    return jnp.dot(left_side, right_side, preferred_element_type=jnp.float32)


def times_transpose(left_side, right_side):
    return lax.dot_general(
        left_side, right_side, (((1,), (1,)), ((), ())), preferred_element_type=jnp.float32
    )


def column_product(left_side, right_side):
    return lax.dot_general(
        left_side, right_side, (((0,), (0,)), ((), ())), preferred_element_type=jnp.float32
    )


def swap(value, axis, count, distance):
    return lax.ppermute(value, axis, [(i, i ^ distance) for i in range(count)])


def gather_tokens(own, count):
    held = own
    distance = count // 2
    while distance:
        held = jnp.concatenate([held, swap(held, "seq", count, distance)])
        distance //= 2
    return held


def scatter_tokens(make, rows, count):
    held = None
    distance = 1
    while distance < count:
        part = rows // 2
        if held is None:
            leave = make(part, rows).astype(low)
            stay = make(0, part)
        else:
            leave = held[part:].astype(low)
            stay = held[:part]
        held = stay + swap(leave, "seq", count, distance).astype(jnp.float32)
        rows = part
        distance *= 2
    return held


def gather_rows(own, member, count, filler):
    blocks = {0: own}
    distance = count // 2
    while distance:
        for k in sorted(blocks):
            blocks[k ^ distance] = swap(blocks[k], "fsdp", count, distance)
        distance //= 2
    lead, rows, columns = own.shape
    result = jnp.broadcast_to(filler, (lead, count, rows, columns))
    for k in range(count):
        result = lax.dynamic_update_slice_in_dim(result, blocks[k][:, None], member ^ k, 1)
    return result.reshape(lead * count * rows, columns)


def scatter_step(value, member, count, remaining, distance):
    lead, rows, columns = value.shape
    above = 2 ** sum(d > distance for d in remaining)
    pairs = value.reshape(lead, above, 2, rows // (2 * above), columns)
    bit = (member // distance) % 2
    leave = lax.dynamic_index_in_dim(pairs, 1 - bit, 2, keepdims=False)
    come = swap(leave.astype(low), "fsdp", count, distance)
    kept = lax.dynamic_index_in_dim(pairs, bit, 2, keepdims=False) + come.astype(jnp.float32)
    return kept.reshape(lead, rows // 2, columns)


def scatter_rows(value, member, count):
    remaining = [2**k for k in range(count.bit_length() - 1)]
    for distance in list(remaining):
        value = scatter_step(value, member, count, remaining, distance)
        remaining = [d for d in remaining if d != distance]
    return value


def scatter_mixed(value, member, count):
    remaining = [2**k for k in range(count.bit_length() - 1)]
    kept = scatter_step(value, member, count, remaining, 1)
    kept = kept.astype(low)
    groups = [[y + 2 * z for z in range(count // 2)] for y in range(2)]
    return lax.psum_scatter(kept, "fsdp", scatter_dimension=1, tiled=True, axis_index_groups=groups)


def total_over_mesh(value, place, counts):
    spots = jnp.arange(8 * 128, dtype=jnp.int32).reshape(8, 128)
    spread = jnp.where(spots == place, value, 0.0)
    for axis, count in counts:
        come = [swap(spread, axis, count, k) for k in range(1, count)]
        for part in come:
            spread = spread + part
    return jnp.sum(spread)


def butterfly(value, counts):
    for axis, count in counts:
        distance = 1
        while distance < count:
            value = value + swap(value, axis, count, distance)
            distance *= 2
    return value


def trade(block_of, member, count):
    return [block_of(member)] + [
        swap(block_of(member ^ k), "seq", count, k) for k in range(1, count)
    ]


def exchange(block_of, member, count):
    pieces = trade(block_of, member, count)
    result = jnp.broadcast_to(pieces[0], (count,) + pieces[0].shape)
    for k, piece in enumerate(pieces):
        result = lax.dynamic_update_slice_in_dim(result, piece[None], member ^ k, 0)
    return lax.optimization_barrier(result)


def visible(query_place, query_segment, places, segments):
    same_segment = (segments[None, :] == query_segment[:, None]) & (
        places[None, :] <= query_place[:, None]
    )
    prompt_shared = (segments[None, :] == 0) & (query_segment[:, None] != 0)
    return same_segment | prompt_shared


def block_scores(queries, key_rows, places, segments, row_start, block_size):
    query_rows = lax.dynamic_slice_in_dim(queries, row_start, block_size, 0)
    allowed = visible(
        lax.dynamic_slice_in_dim(places, row_start, block_size, 0),
        lax.dynamic_slice_in_dim(segments, row_start, block_size, 0),
        places,
        segments,
    )
    scores = jnp.einsum(
        "qhd,kd->hqk", query_rows, key_rows, preferred_element_type=jnp.float32
    ) * queries.shape[2] ** (-0.5)
    return (query_rows, jnp.where(allowed[None], scores, masked_score))


def attend_forward(queries, key_rows, value_rows, places, segments):
    row_total = queries.shape[0]
    block_size = math.gcd(row_total, 512)

    def one_block(row_start):
        _, scores = block_scores(queries, key_rows, places, segments, row_start, block_size)
        top_score = jnp.max(scores, axis=-1, keepdims=True)
        exp_scores = jnp.exp(scores - top_score)
        exp_total = jnp.sum(exp_scores, axis=-1, keepdims=True)
        probs_low = (exp_scores / exp_total).astype(low)
        mixed_out = jnp.einsum(
            "hqk,kd->qhd", probs_low, value_rows, preferred_element_type=jnp.float32
        )
        return (mixed_out.astype(low), (top_score + jnp.log(exp_total))[:, :, 0])

    block_starts = jnp.arange(0, row_total, block_size, dtype=jnp.int32)
    block_outs, logsum = lax.map(one_block, block_starts)
    return (block_outs.reshape(queries.shape), logsum)


def attend_backward(queries, key_rows, value_rows, logsum, grad_out, places, segments):
    row_total = queries.shape[0]
    block_size = math.gcd(row_total, 512)
    scale = queries.shape[2] ** (-0.5)

    def one_block(carry_in, block_item):
        row_start, block_logsum = block_item
        query_rows, scores = block_scores(
            queries, key_rows, places, segments, row_start, block_size
        )
        probs = jnp.exp(scores - block_logsum[:, :, None])
        grad_rows = lax.dynamic_slice_in_dim(grad_out, row_start, block_size, 0)
        grad_probs = jnp.einsum(
            "qhd,kd->hqk", grad_rows, value_rows, preferred_element_type=jnp.float32
        )
        inner_sum = jnp.sum(probs * grad_probs, axis=-1, keepdims=True)
        grad_scores = (probs * (grad_probs - inner_sum)).astype(low)
        query_grad = (
            jnp.einsum("hqk,kd->qhd", grad_scores, key_rows, preferred_element_type=jnp.float32)
            * scale
        )
        key_grad = (
            carry_in[0]
            + jnp.einsum("hqk,qhd->kd", grad_scores, query_rows, preferred_element_type=jnp.float32)
            * scale
        )
        value_grad = carry_in[1] + jnp.einsum(
            "hqk,qhd->kd", probs.astype(low), grad_rows, preferred_element_type=jnp.float32
        )
        return ((key_grad, value_grad), query_grad.astype(low))

    block_starts = jnp.arange(0, row_total, block_size, dtype=jnp.int32)
    zero_grad = jnp.zeros(key_rows.shape, jnp.float32)
    (key_grad, value_grad), query_grads = lax.scan(
        one_block, (zero_grad, zero_grad), (block_starts, logsum)
    )
    return (query_grads.reshape(queries.shape), jnp.concatenate([key_grad, value_grad], axis=1))


def adam_update(master, first, second, gradient, factor):
    clipped = gradient * factor
    first_new = first_decay * first + (1.0 - first_decay) * clipped
    second_new = second_decay * second + (1.0 - second_decay) * clipped * clipped
    first_hat = first_new / (1.0 - first_decay**STEP)
    second_hat = second_new / (1.0 - second_decay**STEP)
    updated = master - learn_rate * (
        first_hat / (jnp.sqrt(second_hat) + adam_epsilon) + decay_rate * master
    )
    return (updated, first_new, second_new)


def fold_kernel(count, widths, extra, scalars, factor_ref, *refs):
    parts = len(widths)
    pieces = [refs[k * parts : (k + 1) * parts] for k in range(count)]
    state = refs[count * parts :]
    factor = factor_ref[0, 0]
    start = 0
    for m in range(count):
        source = scalars[0] ^ m
        for h, width in enumerate(widths):
            gradient = pieces[0][h][:, :width]
            for k in range(1, count):
                gradient = jnp.where(source == k, pieces[k][h][:, :width], gradient)
            put_update(state, start, start + width, gradient, factor)
            start += width
    if extra:
        gradient = pieces[0][0][:, widths[0] :].astype(jnp.float32)
        for k in range(1, count):
            gradient = gradient + pieces[k][0][:, widths[0] :].astype(jnp.float32)
        put_update(state, start, start + extra, gradient, factor)


def put_update(refs, start, stop, gradient, factor):
    master, first, second, updated, first_new, second_new = refs
    state = adam_update(
        master[:, start:stop],
        first[:, start:stop],
        second[:, start:stop],
        gradient.astype(jnp.float32),
        factor,
    )
    updated[:, start:stop] = state[0]
    first_new[:, start:stop] = state[1]
    second_new[:, start:stop] = state[2]


def fold_update(pieces, member, factor, master, first, second, extra):
    count = len(pieces)
    rows, columns = master.shape
    flat = [part for piece in pieces for part in piece]
    widths = [part.shape[1] - extra for part in pieces[0]]
    tile = max(16, rows // 4)
    state_spec = pl.BlockSpec((tile, columns), lambda i, scalars: (i, 0))
    piece_specs = [pl.BlockSpec((tile, p.shape[1]), lambda i, scalars: (i, 0)) for p in flat]
    return pl.pallas_call(
        functools.partial(fold_kernel, count, widths, extra),
        out_shape=[jax.ShapeDtypeStruct(master.shape, jnp.float32)] * 3,
        grid_spec=pltpu.PrefetchScalarGridSpec(
            num_scalar_prefetch=1,
            grid=(rows // tile,),
            in_specs=[pl.BlockSpec(memory_space=pltpu.SMEM)] + piece_specs + [state_spec] * 3,
            out_specs=[state_spec] * 3,
        ),
        name="fold_update",
    )(member.reshape(1), factor.reshape(1, 1), *flat, master, first, second)


def local_step(
    count,
    shard_count,
    hidden_in,
    out_cotangent,
    seg_ids,
    mixer_master,
    mixer_first,
    mixer_second,
    project_master,
    project_first,
    project_second,
    expand_master,
    expand_first,
    expand_second,
    reduce_master,
    reduce_first,
    reduce_second,
    affine_master,
    affine_first,
    affine_second,
):
    member = lax.axis_index("seq")
    shard = lax.axis_index("fsdp")
    shards = shard_count
    counts = (("seq", count), ("fsdp", shards))
    token_count = hidden_in.shape[1]
    group_tokens = token_count * count
    heads = HEADS // count
    width = heads * HEAD
    slab = FF // count
    mixer_low = mixer_master.astype(low)

    def mixer_block(m):
        return jnp.concatenate(
            [lax.dynamic_slice_in_dim(mixer_low, m * width, width, 1), mixer_low[:, D:]], axis=1
        )

    def expand_block(m):
        return lax.dynamic_slice_in_dim(expand_low, m * slab, slab, 1)

    mixer_rows = exchange(mixer_block, member, count)
    project_low = project_master.astype(low)[None]
    mixer_rows, late_expand, late_reduce, seg_ids, hidden_in = lax.optimization_barrier(
        (mixer_rows, expand_master, reduce_master, seg_ids, hidden_in)
    )
    expand_low = late_expand.astype(low)
    hidden = hidden_in[0].astype(jnp.float32)
    segment_rows = seg_ids[0].reshape(count, token_count)
    spans = [0]
    distance = count // 2
    while distance:
        spans = spans + [k ^ distance for k in spans]
        distance //= 2
    owners = [member ^ k for k in spans]
    segments = jnp.concatenate([segment_rows[m] for m in owners])
    places = jnp.concatenate(
        [m * token_count + jnp.arange(token_count, dtype=jnp.int32) for m in owners]
    )

    filler = mixer_rows[0, 0, 0]
    mixer_w = lax.all_gather(mixer_rows, "fsdp", axis=1, tiled=True).reshape(D, width + KV)
    project_w = gather_rows(project_low, shard, shards, filler)
    expand_rows = exchange(expand_block, member, count)
    expand_w = gather_rows(expand_rows, shard, shards, filler)

    ln_one_own = layer_norm(hidden, affine_master[0], affine_master[1]).astype(low)
    ln_one = gather_tokens(ln_one_own, count)
    mixed = product(ln_one, mixer_w).astype(low)
    mixed, reduce_rows = lax.optimization_barrier((mixed, late_reduce.astype(low)))
    reduce_w = lax.all_gather(reduce_rows, "fsdp", axis=0, tiled=True)
    queries = mixed[:, :width].reshape(group_tokens, heads, HEAD)
    key_rows = mixed[:, width : width + HEAD]
    value_rows = mixed[:, width + HEAD :]
    head_out, logsum = attend_forward(queries, key_rows, value_rows, places, segments)
    attended = head_out.reshape(group_tokens, width)

    def project_rows(start, stop):
        return product(attended[start:stop], project_w)

    middle = hidden + scatter_tokens(project_rows, group_tokens, count)
    ln_two = gather_tokens(
        layer_norm(middle, affine_master[2], affine_master[3]).astype(low), count
    )
    cotangent = gather_tokens(out_cotangent[0], count)
    expanded = product(ln_two, expand_w)
    activated = activate(expanded).astype(low)

    reduce_halves = []
    for h in range(2):
        part = column_product(activated, cotangent[:, h * D // 2 : (h + 1) * D // 2])
        reduce_halves.append(scatter_mixed(part[None], shard, shards)[0])
    grad_activated = times_transpose(cotangent, reduce_w)
    _, gelu_pull = jax.vjp(activate, expanded)
    grad_expanded = gelu_pull(grad_activated)[0].astype(low)

    def normed_rows(start, stop):
        return times_transpose(grad_expanded[start:stop], expand_w)

    grad_normed = scatter_tokens(normed_rows, group_tokens, count)
    expand_halves = []
    for h in range(2):
        part = column_product(ln_two, grad_expanded[:, h * slab // 2 : (h + 1) * slab // 2])
        part = scatter_mixed(part.reshape(count, D // count, slab // 2), shard, shards)
        expand_halves.append(trade(lambda m: part[m], member, count))
    expand_pieces = list(zip(*expand_halves))

    _, second_pull = jax.vjp(layer_norm, middle, affine_master[2], affine_master[3])
    grad_inner, gain_two, shift_two = second_pull(grad_normed)
    grad_middle = out_cotangent[0].astype(jnp.float32) + grad_inner
    branch_own = grad_middle.astype(low)
    branch_own, late_activated, late_middle = lax.optimization_barrier(
        (branch_own, activated, middle)
    )
    grad_branch = gather_tokens(branch_own, count)

    def output_rows(start, stop):
        return product(late_activated[start:stop], reduce_w)

    output = late_middle + scatter_tokens(output_rows, group_tokens, count)
    block_output = output.astype(low)[None]
    grad_head = (
        times_transpose(grad_branch, project_w).astype(low).reshape(group_tokens, heads, HEAD)
    )
    project_part = column_product(attended, grad_branch)
    project_grad = scatter_rows(project_part[None], shard, shards)[0]
    query_part, key_value_part = attend_backward(
        queries, key_rows, value_rows, logsum, grad_head, places, segments
    )
    grad_mixed = jnp.concatenate(
        [query_part.reshape(group_tokens, width), key_value_part.astype(low)], axis=1
    )
    mixer_part = column_product(ln_one, grad_mixed)
    mixer_part = scatter_rows(mixer_part.reshape(count, D // count, width + KV), shard, shards)
    mixer_pieces = trade(lambda m: mixer_part[m], member, count)

    def first_rows(start, stop):
        return times_transpose(grad_mixed[start:stop], mixer_w)

    grad_first = scatter_tokens(first_rows, group_tokens, count)
    _, first_pull = jax.vjp(layer_norm, hidden, affine_master[0], affine_master[1])
    grad_hidden, gain_one, shift_one = first_pull(grad_first)
    input_grad = (grad_middle + grad_hidden).astype(low)[None]

    affine_grad = butterfly(jnp.stack([gain_one, shift_one, gain_two, shift_two]), counts)
    expand_squares = [
        jnp.sum(jnp.square(p.astype(jnp.float32))) for ps in [*expand_pieces, reduce_halves] for p in ps
    ]
    mixer_squares = [jnp.sum(jnp.square(p[:, :width])) for p in mixer_pieces]
    shared_grad = sum(p[:, width:] for p in mixer_pieces)
    local_square = (
        sum(mixer_squares)
        + jnp.sum(shared_grad * shared_grad)
        + jnp.sum(project_grad * project_grad)
        + sum(expand_squares)
    )
    square_total = total_over_mesh(local_square, member * shards + shard, counts) + jnp.sum(
        affine_grad * affine_grad
    )
    grad_norm = jnp.sqrt(square_total)
    limit = math.sqrt(float(D * (D + KV) + D * D + 2 * D * FF + 4 * D))
    factor = limit / jnp.maximum(grad_norm, limit)
    mixer_state = fold_update(
        [[p] for p in mixer_pieces], member, factor, mixer_master, mixer_first, mixer_second, KV
    )
    project_state = adam_update(project_master, project_first, project_second, project_grad, factor)
    expand_state = fold_update(
        expand_pieces, member, factor, expand_master, expand_first, expand_second, 0
    )
    reduce_state = fold_update(
        [reduce_halves], member, factor, reduce_master, reduce_first, reduce_second, 0
    )
    affine_state = adam_update(affine_master, affine_first, affine_second, affine_grad, factor)
    return (
        block_output,
        input_grad,
        grad_norm,
        *mixer_state,
        *project_state,
        *expand_state,
        *reduce_state,
        affine_state[0] - affine_master,
        affine_state[1],
        affine_state[2],
    )


def solution(mesh):
    count = mesh.shape["seq"]
    tokens = P("fsdp", "seq", None)
    rows = P(("seq", "fsdp"), None)
    in_specs = (tokens, tokens, P("fsdp", None)) + (rows,) * 12 + (P(),) * 3
    out_specs = (tokens, tokens, P()) + (rows,) * 12 + (P(),) * 3

    def local(*values):
        return local_step(count, mesh.shape["fsdp"], *values)

    return jax.shard_map(local, mesh=mesh, in_specs=in_specs, out_specs=out_specs, check_vma=False)
```

profile of v0, /device:TPU:0, one launch (start us, length us, event | category | flops | bytes accessed | tf_op | source)
XLA Modules:
  0.0 891.4 jit_solution(1563190584443943265)
XLA Ops:
  46.9 10.1 %collective-permute-done.12 = bf16[1,64,2048]{2,1,0:T(8,128)(2,1)S(1)} collective-permute-done((bf16[1,64,2048]{2,1,0:T(8,128)(2,1)}, bf16[1,64,2048]{2,1,0:T(8,128)(2,1)S(1)}, u32[]{:S(2)}, u32[]{:S(2)}) %collective-permute-start.12) | collective-permute-done | bytes 262176 | tf_op jit(solution)/shard_map/ppermute | solution.py:56
  58.5 17.0 %collective-permute-done.5 = bf16[256,2048]{1,0:T(8,128)(2,1)} collective-permute-done((bf16[256,2048]{1,0:T(8,128)(2,1)}, bf16[256,2048]{1,0:T(8,128)(2,1)}, u32[]{:S(2)}, u32[]{:S(2)}) %collective-permute-start.5) | collective-permute-done | bytes 1048608 | tf_op jit(solution)/shard_map/ppermute | solution.py:56
  82.0 11.1 %all-gather.3.cloned.1.call-done = bf16[4,512,768]{2,1,0:T(8,128)(2,1)} async-done(((bf16[4,64,768]{2,1,0:T(8,128)(2,1)}), bf16[4,512,768]{2,1,0:T(8,128)(2,1)}) %all-gather.3.cloned.1.call-update) | async-done | bytes 3145744 | tf_op jit(solution)/shard_map/all_gather | solution.py:369
  93.1 6.6 fusion.95
  99.9 23.9 %while.27 = (s32[]{:T(128)}, bf16[2,512,4,128]{3,1,2,0:T(8,128)(2,1)}, f32[2,4,512]{2,1,0:T(4,128)}, s32[1024]{0:T(1024)S(1)}, s32[2]{0:T(128)S(1)}, /*index=5*/...) while((s32[]{:T(128)}, ...), condition=%wide.region_5.6_spmd, body=%wide.region_2.5_spmd.sunk | while | flops 1101790720 | bytes 37317876 | solution.py:197
  128.7 4.2 convolution_convert_fusion.3
  139.8 4.8 collective-permute-done.19
  164.9 60.2 %collective-permute-done.24 = bf16[4,64,2048]{2,1,0:T(8,128)(2,1)} collective-permute-done((bf16[4,64,2048]{2,1,0:T(8,128)(2,1)}, bf16[4,64,2048]{2,1,0:T(8,128)(2,1)}, u32[]{:S(2)}, u32[]{:S(2)}) %collective-permute-start.24) | collective-permute-done | bytes 1048608 | tf_op jit(solution)/shard_map/ppermute | solution.py:56
  227.1 4.0 collective-permute-start.26
  238.2 50.9 %collective-permute-done.26 = bf16[4,64,2048]{2,1,0:T(8,128)(2,1)S(1)} collective-permute-done((bf16[4,64,2048]{2,1,0:T(8,128)(2,1)}, bf16[4,64,2048]{2,1,0:T(8,128)(2,1)S(1)}, u32[]{:S(2)}, u32[]{:S(2)}) %collective-permute-start.26) | collective-permute-done | bytes 1048608 | tf_op jit(solution)/shard_map/ppermute | solution.py:56
  290.6 27.0 %collective-permute-done.23 = bf16[4,64,2048]{2,1,0:T(8,128)(2,1)S(1)} collective-permute-done((bf16[4,64,2048]{2,1,0:T(8,128)(2,1)}, bf16[4,64,2048]{2,1,0:T(8,128)(2,1)S(1)}, u32[]{:S(2)}, u32[]{:S(2)}) %collective-permute-start.23) | collective-permute-done | bytes 1048608 | tf_op jit(solution)/shard_map/ppermute | solution.py:56
  322.2 17.5 %collective-permute-done.27 = bf16[4,64,2048]{2,1,0:T(8,128)(2,1)S(1)} collective-permute-done((bf16[4,64,2048]{2,1,0:T(8,128)(2,1)S(1)}, bf16[4,64,2048]{2,1,0:T(8,128)(2,1)S(1)}, u32[]{:S(2)}, u32[]{:S(2)}) %collective-permute-start.27) | collective-permute-done | bytes 1048608 | tf_op jit(solution)/shard_map/ppermute | solution.py:56
  339.9 4.0 copy-done.99
  343.9 14.1 %multiply_convert_fusion = (bf16[1024,2048]{1,0:T(8,128)(2,1)S(1)}, f32[1024,2048]{1,0:T(8,128)}) fusion(bf16[2048,2048]{1,0:T(8,128)(2,1)S(1)} %bitcast.408, bf16[512,2048]{1,0:T(8,128)(2,1)} %copy-done.99, bf16[256,2048]{1,0:T(8,128)(2,1)S(1)} %collective-permute-done.16, bf16[256,2048]{1,0:T(8,128)(2,1)S(1)} %add_convert_fusion.1), kind=kOutput, calls=%fused_computation.68 | convolution fusion | flops 8621391872 | bytes 25165824 | tf_op jit(solution)/shard_map/dot_general | solution.py:40
  358.0 4.7 fusion.78
  368.0 7.2 fusion.76
  381.8 34.7 %collective-permute-done.53 = bf16[1,4,256,1024]{3,2,1,0:T(8,128)(2,1)} collective-permute-done((bf16[1,4,256,1024]{3,2,1,0:T(8,128)(2,1)}, bf16[1,4,256,1024]{3,2,1,0:T(8,128)(2,1)}, u32[]{:S(2)}, u32[]{:S(2)}) %collective-permute-start.53) | collective-permute-done | bytes 2097184 | tf_op jit(solution)/shard_map/ppermute | solution.py:56
  420.3 20.7 %fusion.52 = bf16[1024,2048]{1,0:T(8,128)(2,1)} fusion(f32[1024,2048]{1,0:T(8,128)} %get-tuple-element.405, bf16[2048,2048]{1,0:T(8,128)(2,1)} %all-gather.5.cloned.1.call-done, bf16[512,2048]{1,0:T(8,128)(2,1)} %copy-done.47, bf16[256,2048]{1,0:T(8,128)(2,1)} %collective-permute-done, bf16[256,2048]{1,0:T(8,128)(2,1)S(1)} %bitcast.405), kind=kOutput, calls=%fused_computation.67 | convolution fusion | flops 8644460544 | bytes 25165824 | tf_op jit(solution)/shard_map/dot_general | solution.py:44
  441.0 9.9 %convolution_convert_fusion.2 = bf16[512,2048]{1,0:T(8,128)(2,1)} fusion(bf16[2048,2048]{1,0:T(8,128)(2,1)} %bitcast.409, bf16[1024,2048]{1,0:T(8,128)(2,1)} %fusion.52), kind=kOutput, calls=%fused_computation.96 | convolution fusion | flops 4296015872 | bytes 12582912 | tf_op jit(solution)/shard_map/dot_general | solution.py:44
  451.0 9.4 %collective-permute-done.54 = bf16[1,4,256,1024]{3,2,1,0:T(8,128)(2,1)} collective-permute-done((bf16[1,4,256,1024]{3,2,1,0:T(8,128)(2,1)}, bf16[1,4,256,1024]{3,2,1,0:T(8,128)(2,1)}, u32[]{:S(2)}, u32[]{:S(2)}) %collective-permute-start.54) | collective-permute-done | bytes 2097184 | tf_op jit(solution)/shard_map/ppermute | solution.py:56
  460.3 5.0 fusion.55
  465.4 7.4 fusion.82
  473.5 9.3 %convert_add_fusion.2 = f32[512,2048]{1,0:T(8,128)S(1)} fusion(bf16[512,2048]{1,0:T(8,128)(2,1)} %collective-permute-done.28, bf16[2048,2048]{1,0:T(8,128)(2,1)} %bitcast.410, bf16[1024,2048]{1,0:T(8,128)(2,1)} %fusion.52), kind=kOutput, calls=%fused_computation.88 | convolution fusion | flops 4297064448 | bytes 16777216 | tf_op jit(solution)/shard_map/dot_general | solution.py:44
  485.6 7.0 fusion.80
  496.0 25.8 %collective-permute-done.45 = bf16[4,4,64,1024]{3,2,1,0:T(8,128)(2,1)} collective-permute-done((bf16[4,4,64,1024]{3,2,1,0:T(8,128)(2,1)S(1)}, bf16[4,4,64,1024]{3,2,1,0:T(8,128)(2,1)}, u32[]{:S(2)}, u32[]{:S(2)}) %collective-permute-start.45) | collective-permute-done | bytes 2097184 | tf_op jit(solution)/shard_map/ppermute | solution.py:56
  521.8 3.8 fusion.58
  533.1 9.5 %convolution_convert_fusion.1 = bf16[512,2048]{1,0:T(8,128)(2,1)} fusion(bf16[2048,2048]{1,0:T(8,128)(2,1)} %all-gather.5.cloned.1.call-done, bf16[1024,2048]{1,0:T(8,128)(2,1)S(1)} %copy-done.103), kind=kOutput, calls=%fused_computation.95 | convolution fusion | flops 4296015872 | bytes 12582912 | tf_op jit(solution)/shard_map/dot_general | solution.py:40
  550.3 14.4 %collective-permute-done.46 = bf16[4,4,64,1024]{3,2,1,0:T(8,128)(2,1)} collective-permute-done((bf16[4,4,64,1024]{3,2,1,0:T(8,128)(2,1)}, bf16[4,4,64,1024]{3,2,1,0:T(8,128)(2,1)}, u32[]{:S(2)}, u32[]{:S(2)}) %collective-permute-start.46) | collective-permute-done | bytes 2097184 | tf_op jit(solution)/shard_map/ppermute | solution.py:56
  564.7 5.0 fusion.57
  572.9 8.6 convert_add_fusion.1
  583.1 6.7 convolution_convert_fusion.4
  589.9 50.7 %while.28 = (s32[]{:T(128)}, f32[1024,128]{1,0:T(8,128)S(1)}, f32[1024,128]{1,0:T(8,128)S(1)}, bf16[2,512,4,128]{3,2,1,0:T(4,128)(2,1)}, s32[1024]{0:T(1024)S(1)...) while((s32[]{:T(128)}, f32[1024,128]{1,0:T(8,128)S(1)}, ...), condition=%wide.region_12.13_spmd.clone, body=%wide.region_10.12_spmd.clone.sunk | while | flops 2719612416 | bytes 138759600 | solution.py:234
  594.7 4.0 fusion.187
  606.2 6.3 fusion.190
  619.9 4.0 fusion.187
  631.4 6.3 fusion.190
  642.2 5.5 fusion.93
  671.5 36.0 %collective-permute-done.42 = bf16[1,4,64,2048]{3,2,1,0:T(8,128)(2,1)} collective-permute-done((bf16[1,4,64,2048]{3,2,1,0:T(8,128)(2,1)}, bf16[1,4,64,2048]{3,2,1,0:T(8,128)(2,1)}, u32[]{:S(2)}, u32[]{:S(2)}) %collective-permute-start.42) | collective-permute-done | bytes 1048608 | tf_op jit(solution)/shard_map/ppermute | solution.py:56
  715.8 9.7 %collective-permute-done.43 = bf16[1,2,64,2048]{3,2,1,0:T(8,128)(2,1)S(1)} collective-permute-done((bf16[1,2,64,2048]{3,2,1,0:T(8,128)(2,1)S(1)}, bf16[1,2,64,2048]{3,2,1,0:T(8,128)(2,1)S(1)}, u32[]{:S(2)}, u32[]{:S(2)}) %collective-permute-start.43) | collective-permute-done | bytes 524320 | tf_op jit(solution)/shard_map/ppermute | solution.py:56
  726.4 15.7 %collective-permute-done.37 = bf16[4,2,64,768]{3,2,1,0:T(8,128)(2,1)S(1)} collective-permute-done((bf16[4,2,64,768]{3,2,1,0:T(8,128)(2,1)S(1)}, bf16[4,2,64,768]{3,2,1,0:T(8,128)(2,1)S(1)}, u32[]{:S(2)}, u32[]{:S(2)}) %collective-permute-start.37) | collective-permute-done | bytes 786464 | tf_op jit(solution)/shard_map/ppermute | solution.py:56
  753.2 13.3 %collective-permute-done.44 = bf16[1,1,64,2048]{3,2,1,0:T(8,128)(2,1)S(1)} collective-permute-done((bf16[1,1,64,2048]{3,2,1,0:T(8,128)(2,1)}, bf16[1,1,64,2048]{3,2,1,0:T(8,128)(2,1)S(1)}, u32[]{:S(2)}, u32[]{:S(2)}) %collective-permute-start.44) | collective-permute-done | bytes 262176 | tf_op jit(solution)/shard_map/ppermute | solution.py:56
  767.2 6.8 collective-permute-done.38
  776.0 4.4 convert_add_fusion
  788.1 26.0 %collective-permute-done.40.refs_2_ = f32[64,768]{1,0:T(8,128)} collective-permute-done((f32[64,768]{1,0:T(8,128)}, f32[64,768]{1,0:T(8,128)}, u32[]{:S(2)}, u32[]{:S(2)}) %collective-permute-start.40) | collective-permute-done | bytes 196640 | tf_op jit(solution)/shard_map/ppermute | solution.py:56
  831.6 3.9 collective-permute-start.61
  863.7 6.9 fold_update.5
  870.6 4.1 fold_update.3
  876.1 6.8 fold_update.4
  (549 shorter events, 273.4 us)
Async XLA Ops:
  7.2 85.9 %all-gather.3.cloned.1.call-start = ((), (), s32[]{:S(2)}) async-start(), calls=%async_computation.4 | async-start | bytes 3538944 | tf_op jit(solution)/shard_map/all_gather | solution.py:369
  9.1 32.5 %collective-permute-start.7 = (bf16[1,64,2048]{2,1,0:T(8,128)(2,1)}, bf16[1,64,2048]{2,1,0:T(8,128)(2,1)}, u32[]{:S(2)}, u32[]{:S(2)}) collective-permute-start(bf16[1,64,2048]{2,1,0:T(8,128)(2,1)} %convert_bitcast_fusion.1), channel_id=1, source_target_pairs={{0,1},{1,0},{2,3},{3,2},{4,5},{5,4},{6,7},{7,6},{8,9},{9,8},{10,11... | collective-permute-start | bytes 786440 | tf_op jit(solution)/shard_map/ppermute | solution.py:56
  12.1 30.0 %collective-permute-start.8 = (bf16[1,64,2048]{2,1,0:T(8,128)(2,1)}, bf16[1,64,2048]{2,1,0:T(8,128)(2,1)}, u32[]{:S(2)}, u32[]{:S(2)}) collective-permute-start(bf16[1,64,2048]{2,1,0:T(8,128)(2,1)} %convert_bitcast_fusion.1), channel_id=1, source_target_pairs={{0,2},{1,3},{2,0},{3,1},{4,6},{5,7},{6,4},{7,5},{8,10},{9,11},{10,... | collective-permute-start | bytes 786440 | tf_op jit(solution)/shard_map/ppermute | solution.py:56
  13.7 27.4 %collective-permute-start.10 = (bf16[1,64,2048]{2,1,0:T(8,128)(2,1)}, bf16[1,64,2048]{2,1,0:T(8,128)(2,1)}, u32[]{:S(2)}, u32[]{:S(2)}) collective-permute-start(bf16[1,64,2048]{2,1,0:T(8,128)(2,1)} %convert_bitcast_fusion.1), channel_id=1, source_target_pairs={{0,4},{1,5},{2,6},{3,7},{4,0},{5,1},{6,2},{7,3},{8,12},{9,13},{10,... | collective-permute-start | bytes 786440 | tf_op jit(solution)/shard_map/ppermute | solution.py:56
  26.5 136.6 %collective-permute-start = (bf16[256,2048]{1,0:T(8,128)(2,1)}, bf16[256,2048]{1,0:T(8,128)(2,1)}, u32[]{:S(2)}, u32[]{:S(2)}) collective-permute-start(bf16[256,2048]{1,0:T(8,128)(2,1)} %bitcast.402), channel_id=1, source_target_pairs={{0,16},{8,24},{16,0},{24,8},{1,17},{9,25},{17,1},{25,9},{2,18},{10... | collective-permute-start | bytes 3145736 | tf_op jit(solution)/shard_map/ppermute | solution.py:56
  30.9 389.4 %all-gather.5.cloned.1.call-start = ((), (), s32[]{:S(2)}) async-start(), calls=%async_computation.5 | async-start | bytes 9437184 | tf_op jit(solution)/shard_map/all_gather | solution.py:378
  35.1 40.4 %collective-permute-start.5 = (bf16[256,2048]{1,0:T(8,128)(2,1)}, bf16[256,2048]{1,0:T(8,128)(2,1)}, u32[]{:S(2)}, u32[]{:S(2)}) collective-permute-start(bf16[256,2048]{1,0:T(8,128)(2,1)} %fusion.68), channel_id=1, source_target_pairs={{0,16},{8,24},{16,0},{24,8},{1,17},{9,25},{17,1},{25,9},{2,18},{10... | collective-permute-start | bytes 3145736 | tf_op jit(solution)/shard_map/ppermute | solution.py:56
  41.0 38.8 %collective-permute-start.11 = (bf16[1,64,2048]{2,1,0:T(8,128)(2,1)}, bf16[1,64,2048]{2,1,0:T(8,128)(2,1)S(1)}, u32[]{:S(2)}, u32[]{:S(2)}) collective-permute-start(bf16[1,64,2048]{2,1,0:T(8,128)(2,1)} %collective-permute-done.10), channel_id=1, source_target_pairs={{0,1},{1,0},{2,3},{3,2},{4,5},{5,4},{6,7},{7,6},{8,9},{9,8},{10,11... | collective-permute-start | bytes 786440 | tf_op jit(solution)/shard_map/ppermute | solution.py:56
  42.1 35.3 %collective-permute-start.9 = (bf16[1,64,2048]{2,1,0:T(8,128)(2,1)}, bf16[1,64,2048]{2,1,0:T(8,128)(2,1)S(1)}, u32[]{:S(2)}, u32[]{:S(2)}) collective-permute-start(bf16[1,64,2048]{2,1,0:T(8,128)(2,1)} %collective-permute-done.8), channel_id=1, source_target_pairs={{0,1},{1,0},{2,3},{3,2},{4,5},{5,4},{6,7},{7,6},{8,9},{9,8},{10,11... | collective-permute-start | bytes 786440 | tf_op jit(solution)/shard_map/ppermute | solution.py:56
  57.0 24.2 %collective-permute-start.13 = (bf16[1,64,2048]{2,1,0:T(8,128)(2,1)S(1)}, bf16[1,64,2048]{2,1,0:T(8,128)(2,1)S(1)}, u32[]{:S(2)}, u32[]{:S(2)}) collective-permute-start(bf16[1,64,2048]{2,1,0:T(8,128)(2,1)S(1)} %collective-permute-done.12), channel_id=1, source_target_pairs={{0,1},{1,0},{2,3},{3,2},{4,5},{5,4},{6,7},{7,6},{8,9},{9,8},{10,11... | collective-permute-start | bytes 786440 | tf_op jit(solution)/shard_map/ppermute | solution.py:56
  132.9 18.8 %collective-permute-start.14 = (bf16[512,2048]{1,0:T(8,128)(2,1)}, bf16[512,2048]{1,0:T(8,128)(2,1)}, u32[]{:S(2)}, u32[]{:S(2)}) collective-permute-start(bf16[512,2048]{1,0:T(8,128)(2,1)} %convolution_convert_fusion.3), channel_id=1, source_target_pairs={{0,8},{8,0},{16,24},{24,16},{1,9},{9,1},{17,25},{25,17},{2,10},{10... | collective-permute-start | bytes 6291464 | tf_op jit(solution)/shard_map/ppermute | solution.py:56
  136.9 409.5 %reduce-scatter.9.cloned.1.call-start = ((), (), s32[]{:S(2)}) async-start(), calls=%async_computation.8 | async-start | bytes 2621440 | tf_op jit(solution)/shard_map/reduce_scatter | solution.py:123
  149.1 78.0 %collective-permute-start.22 = (bf16[4,64,2048]{2,1,0:T(8,128)(2,1)}, bf16[4,64,2048]{2,1,0:T(8,128)(2,1)}, u32[]{:S(2)}, u32[]{:S(2)}) collective-permute-start(bf16[4,64,2048]{2,1,0:T(8,128)(2,1)} %bitcast_dynamic-update-slice_fusion.9), channel_id=1, source_target_pairs={{0,2},{1,3},{2,0},{3,1},{4,6},{5,7},{6,4},{7,5},{8,10},{9,11},{10,... | collective-permute-start | bytes 3145736 | tf_op jit(solution)/shard_map/ppermute | solution.py:56
  150.6 74.5 %collective-permute-start.24 = (bf16[4,64,2048]{2,1,0:T(8,128)(2,1)}, bf16[4,64,2048]{2,1,0:T(8,128)(2,1)}, u32[]{:S(2)}, u32[]{:S(2)}) collective-permute-start(bf16[4,64,2048]{2,1,0:T(8,128)(2,1)} %bitcast_dynamic-update-slice_fusion.9), channel_id=1, source_target_pairs={{0,4},{1,5},{2,6},{3,7},{4,0},{5,1},{6,2},{7,3},{8,12},{9,13},{10,... | collective-permute-start | bytes 3145736 | tf_op jit(solution)/shard_map/ppermute | solution.py:56
  157.5 73.7 %collective-permute-start.15 = (bf16[256,2048]{1,0:T(8,128)(2,1)S(1)}, bf16[256,2048]{1,0:T(8,128)(2,1)S(1)}, u32[]{:S(2)}, u32[]{:S(2)}) collective-permute-start(bf16[256,2048]{1,0:T(8,128)(2,1)S(1)} %slice.276), channel_id=1, source_target_pairs={{0,16},{8,24},{16,0},{24,8},{1,17},{9,25},{17,1},{25,9},{2,18},{10... | collective-permute-start | bytes 3145736 | tf_op jit(solution)/shard_map/ppermute | solution.py:56
  159.0 76.2 %collective-permute-start.21 = (bf16[4,64,2048]{2,1,0:T(8,128)(2,1)}, bf16[4,64,2048]{2,1,0:T(8,128)(2,1)S(1)}, u32[]{:S(2)}, u32[]{:S(2)}) collective-permute-start(bf16[4,64,2048]{2,1,0:T(8,128)(2,1)} %bitcast_dynamic-update-slice_fusion.9), channel_id=1, source_target_pairs={{0,1},{1,0},{2,3},{3,2},{4,5},{5,4},{6,7},{7,6},{8,9},{9,8},{10,11... | collective-permute-start | bytes 3145736 | tf_op jit(solution)/shard_map/ppermute | solution.py:56
  164.5 155.4 %collective-permute-start.1 = (bf16[512,2048]{1,0:T(8,128)(2,1)S(1)}, bf16[512,2048]{1,0:T(8,128)(2,1)S(1)}, u32[]{:S(2)}, u32[]{:S(2)}) collective-permute-start(bf16[512,2048]{1,0:T(8,128)(2,1)S(1)} %pad_maximum_fusion.3), channel_id=1, source_target_pairs={{0,8},{8,0},{16,24},{24,16},{1,9},{9,1},{17,25},{25,17},{2,10},{10... | collective-permute-start | bytes 6291464 | tf_op jit(solution)/shard_map/ppermute | solution.py:56
  225.1 94.5 %collective-permute-start.25 = (bf16[4,64,2048]{2,1,0:T(8,128)(2,1)}, bf16[4,64,2048]{2,1,0:T(8,128)(2,1)S(1)}, u32[]{:S(2)}, u32[]{:S(2)}) collective-permute-start(bf16[4,64,2048]{2,1,0:T(8,128)(2,1)} %collective-permute-done.24), channel_id=1, source_target_pairs={{0,1},{1,0},{2,3},{3,2},{4,5},{5,4},{6,7},{7,6},{8,9},{9,8},{10,11... | collective-permute-start | bytes 3145736 | tf_op jit(solution)/shard_map/ppermute | solution.py:56
  227.1 62.0 %collective-permute-start.26 = (bf16[4,64,2048]{2,1,0:T(8,128)(2,1)}, bf16[4,64,2048]{2,1,0:T(8,128)(2,1)S(1)}, u32[]{:S(2)}, u32[]{:S(2)}) collective-permute-start(bf16[4,64,2048]{2,1,0:T(8,128)(2,1)} %collective-permute-done.24), channel_id=1, source_target_pairs={{0,2},{1,3},{2,0},{3,1},{4,6},{5,7},{6,4},{7,5},{8,10},{9,11},{10,... | collective-permute-start | bytes 3145736 | tf_op jit(solution)/shard_map/ppermute | solution.py:56
  232.1 85.5 %collective-permute-start.23 = (bf16[4,64,2048]{2,1,0:T(8,128)(2,1)}, bf16[4,64,2048]{2,1,0:T(8,128)(2,1)S(1)}, u32[]{:S(2)}, u32[]{:S(2)}) collective-permute-start(bf16[4,64,2048]{2,1,0:T(8,128)(2,1)} %collective-permute-done.22), channel_id=1, source_target_pairs={{0,1},{1,0},{2,3},{3,2},{4,5},{5,4},{6,7},{7,6},{8,9},{9,8},{10,11... | collective-permute-start | bytes 3145736 | tf_op jit(solution)/shard_map/ppermute | solution.py:56
  235.2 82.5 %collective-permute-start.16 = (bf16[256,2048]{1,0:T(8,128)(2,1)S(1)}, bf16[256,2048]{1,0:T(8,128)(2,1)S(1)}, u32[]{:S(2)}, u32[]{:S(2)}) collective-permute-start(bf16[256,2048]{1,0:T(8,128)(2,1)S(1)} %add_convert_fusion.1), channel_id=1, source_target_pairs={{0,16},{8,24},{16,0},{24,8},{1,17},{9,25},{17,1},{25,9},{2,18},{10... | collective-permute-start | bytes 3145736 | tf_op jit(solution)/shard_map/ppermute | solution.py:56
  289.1 50.6 %collective-permute-start.27 = (bf16[4,64,2048]{2,1,0:T(8,128)(2,1)S(1)}, bf16[4,64,2048]{2,1,0:T(8,128)(2,1)S(1)}, u32[]{:S(2)}, u32[]{:S(2)}) collective-permute-start(bf16[4,64,2048]{2,1,0:T(8,128)(2,1)S(1)} %collective-permute-done.26), channel_id=1, source_target_pairs={{0,1},{1,0},{2,3},{3,2},{4,5},{5,4},{6,7},{7,6},{8,9},{9,8},{10,11... | collective-permute-start | bytes 3145736 | tf_op jit(solution)/shard_map/ppermute | solution.py:56
  318.0 21.9 %collective-permute-start.17 = (bf16[512,2048]{1,0:T(8,128)(2,1)S(1)}, bf16[512,2048]{1,0:T(8,128)(2,1)S(1)}, u32[]{:S(2)}, u32[]{:S(2)}) collective-permute-start(bf16[512,2048]{1,0:T(8,128)(2,1)S(1)} %pad_maximum_fusion.5), channel_id=1, source_target_pairs={{0,8},{8,0},{16,24},{24,16},{1,9},{9,1},{17,25},{25,17},{2,10},{10... | collective-permute-start | bytes 6291464 | tf_op jit(solution)/shard_map/ppermute | solution.py:56
  367.7 48.8 %collective-permute-start.53 = (bf16[1,4,256,1024]{3,2,1,0:T(8,128)(2,1)}, bf16[1,4,256,1024]{3,2,1,0:T(8,128)(2,1)}, u32[]{:S(2)}, u32[]{:S(2)}) collective-permute-start(bf16[1,4,256,1024]{3,2,1,0:T(8,128)(2,1)} %fusion.74), channel_id=1, source_target_pairs={{0,1},{1,0},{2,3},{3,2},{4,5},{5,4},{6,7},{7,6},{8,9},{9,8},{10,11... | collective-permute-start | bytes 6291464 | tf_op jit(solution)/shard_map/ppermute | solution.py:56
  380.1 80.2 %collective-permute-start.54 = (bf16[1,4,256,1024]{3,2,1,0:T(8,128)(2,1)}, bf16[1,4,256,1024]{3,2,1,0:T(8,128)(2,1)}, u32[]{:S(2)}, u32[]{:S(2)}) collective-permute-start(bf16[1,4,256,1024]{3,2,1,0:T(8,128)(2,1)} %fusion.75), channel_id=1, source_target_pairs={{0,1},{1,0},{2,3},{3,2},{4,5},{5,4},{6,7},{7,6},{8,9},{9,8},{10,11... | collective-permute-start | bytes 6291464 | tf_op jit(solution)/shard_map/ppermute | solution.py:56
  420.2 128.2 %reduce-scatter.11.cloned.1.call-start = ((), (), s32[]{:S(2)}) async-start(), calls=%async_computation.9 | async-start | bytes 2621440 | tf_op jit(solution)/shard_map/reduce_scatter | solution.py:123
  450.9 22.6 %collective-permute-start.28 = (bf16[512,2048]{1,0:T(8,128)(2,1)}, bf16[512,2048]{1,0:T(8,128)(2,1)}, u32[]{:S(2)}, u32[]{:S(2)}) collective-permute-start(bf16[512,2048]{1,0:T(8,128)(2,1)} %convolution_convert_fusion.2), channel_id=1, source_target_pairs={{0,8},{8,0},{16,24},{24,16},{1,9},{9,1},{17,25},{25,17},{2,10},{10... | collective-permute-start | bytes 6291464 | tf_op jit(solution)/shard_map/ppermute | solution.py:56
  465.3 193.0 %reduce-scatter.5.cloned.1.call-start = ((), (), s32[]{:S(2)}) async-start(), calls=%async_computation.6 | async-start | bytes 2621440 | tf_op jit(solution)/shard_map/reduce_scatter | solution.py:123
  473.1 48.7 %collective-permute-start.45 = (bf16[4,4,64,1024]{3,2,1,0:T(8,128)(2,1)S(1)}, bf16[4,4,64,1024]{3,2,1,0:T(8,128)(2,1)}, u32[]{:S(2)}, u32[]{:S(2)}) collective-permute-start(bf16[4,4,64,1024]{3,2,1,0:T(8,128)(2,1)S(1)} %fusion.72), channel_id=1, source_target_pairs={{0,1},{1,0},{2,3},{3,2},{4,5},{5,4},{6,7},{7,6},{8,9},{9,8},{10,11... | collective-permute-start | bytes 6291464 | tf_op jit(solution)/shard_map/ppermute | solution.py:56
  484.1 41.6 %collective-permute-start.29 = (bf16[256,2048]{1,0:T(8,128)(2,1)}, bf16[256,2048]{1,0:T(8,128)(2,1)}, u32[]{:S(2)}, u32[]{:S(2)}) collective-permute-start(bf16[256,2048]{1,0:T(8,128)(2,1)} %slice.275), channel_id=1, source_target_pairs={{0,16},{8,24},{16,0},{24,8},{1,17},{9,25},{17,1},{25,9},{2,18},{10... | collective-permute-start | bytes 3145736 | tf_op jit(solution)/shard_map/ppermute | solution.py:56
  494.5 70.3 %collective-permute-start.46 = (bf16[4,4,64,1024]{3,2,1,0:T(8,128)(2,1)}, bf16[4,4,64,1024]{3,2,1,0:T(8,128)(2,1)}, u32[]{:S(2)}, u32[]{:S(2)}) collective-permute-start(bf16[4,4,64,1024]{3,2,1,0:T(8,128)(2,1)} %fusion.73), channel_id=1, source_target_pairs={{0,1},{1,0},{2,3},{3,2},{4,5},{5,4},{6,7},{7,6},{8,9},{9,8},{10,11... | collective-permute-start | bytes 6291464 | tf_op jit(solution)/shard_map/ppermute | solution.py:56
  525.6 135.0 %reduce-scatter.7.cloned.1.call-start = ((), (), s32[]{:S(2)}) async-start(), calls=%async_computation.7 | async-start | bytes 2621440 | tf_op jit(solution)/shard_map/reduce_scatter | solution.py:123
  542.6 30.2 %collective-permute-start.30 = (bf16[512,2048]{1,0:T(8,128)(2,1)}, bf16[512,2048]{1,0:T(8,128)(2,1)}, u32[]{:S(2)}, u32[]{:S(2)}) collective-permute-start(bf16[512,2048]{1,0:T(8,128)(2,1)} %convolution_convert_fusion.1), channel_id=1, source_target_pairs={{0,8},{8,0},{16,24},{24,16},{1,9},{9,1},{17,25},{25,17},{2,10},{10... | collective-permute-start | bytes 6291464 | tf_op jit(solution)/shard_map/ppermute | solution.py:56
  542.6 27.2 %collective-permute-start.32 = (bf16[256,2048]{1,0:T(8,128)(2,1)S(1)}, bf16[256,2048]{1,0:T(8,128)(2,1)}, u32[]{:S(2)}, u32[]{:S(2)}) collective-permute-start(bf16[256,2048]{1,0:T(8,128)(2,1)S(1)} %fusion.97), channel_id=1, source_target_pairs={{0,16},{8,24},{16,0},{24,8},{1,17},{9,25},{17,1},{25,9},{2,18},{10... | collective-permute-start | bytes 3145736 | tf_op jit(solution)/shard_map/ppermute | solution.py:56
  647.9 62.7 %collective-permute-start.36 = (bf16[4,4,64,768]{3,2,1,0:T(8,128)(2,1)S(1)}, bf16[4,4,64,768]{3,2,1,0:T(8,128)(2,1)S(1)}, u32[]{:S(2)}, u32[]{:S(2)}) collective-permute-start(bf16[4,4,64,768]{3,2,1,0:T(8,128)(2,1)S(1)} %fusion.96), channel_id=1, source_target_pairs={{0,1},{1,0},{2,3},{3,2},{4,5},{5,4},{6,7},{7,6},{8,9},{9,8},{10,11... | collective-permute-start | bytes 4718600 | tf_op jit(solution)/shard_map/ppermute | solution.py:56
  653.4 54.1 %collective-permute-start.42 = (bf16[1,4,64,2048]{3,2,1,0:T(8,128)(2,1)}, bf16[1,4,64,2048]{3,2,1,0:T(8,128)(2,1)}, u32[]{:S(2)}, u32[]{:S(2)}) collective-permute-start(bf16[1,4,64,2048]{3,2,1,0:T(8,128)(2,1)} %fusion.99), channel_id=1, source_target_pairs={{0,1},{1,0},{2,3},{3,2},{4,5},{5,4},{6,7},{7,6},{8,9},{9,8},{10,11... | collective-permute-start | bytes 3145736 | tf_op jit(solution)/shard_map/ppermute | solution.py:56
  658.3 117.6 %collective-permute-start.34 = (bf16[512,2048]{1,0:T(8,128)(2,1)}, bf16[512,2048]{1,0:T(8,128)(2,1)}, u32[]{:S(2)}, u32[]{:S(2)}) collective-permute-start(bf16[512,2048]{1,0:T(8,128)(2,1)} %convolution_convert_fusion), channel_id=1, source_target_pairs={{0,8},{8,0},{16,24},{24,16},{1,9},{9,1},{17,25},{25,17},{2,10},{10... | collective-permute-start | bytes 6291464 | tf_op jit(solution)/shard_map/ppermute | solution.py:56
  668.0 46.6 %collective-permute-start.49 = (bf16[64,1024]{1,0:T(8,128)(2,1)}, bf16[64,1024]{1,0:T(8,128)(2,1)S(1)}, u32[]{:S(2)}, u32[]{:S(2)}) collective-permute-start(bf16[64,1024]{1,0:T(8,128)(2,1)} %get-tuple-element.386), channel_id=1, source_target_pairs={{0,16},{8,24},{16,0},{24,8},{1,17},{9,25},{17,1},{25,9},{2,18},{10... | collective-permute-start | bytes 393224 | tf_op jit(solution)/shard_map/ppermute | solution.py:56
  670.3 74.5 %collective-permute-start.50 = (bf16[64,1024]{1,0:T(8,128)(2,1)}, bf16[64,1024]{1,0:T(8,128)(2,1)S(1)}, u32[]{:S(2)}, u32[]{:S(2)}) collective-permute-start(bf16[64,1024]{1,0:T(8,128)(2,1)} %get-tuple-element.383), channel_id=1, source_target_pairs={{0,16},{8,24},{16,0},{24,8},{1,17},{9,25},{17,1},{25,9},{2,18},{10... | collective-permute-start | bytes 393224 | tf_op jit(solution)/shard_map/ppermute | solution.py:56
  707.4 41.3 %collective-permute-start.51 = (bf16[64,1024]{1,0:T(8,128)(2,1)}, bf16[64,1024]{1,0:T(8,128)(2,1)S(1)}, u32[]{:S(2)}, u32[]{:S(2)}) collective-permute-start(bf16[64,1024]{1,0:T(8,128)(2,1)} %get-tuple-element.385), channel_id=1, source_target_pairs={{0,24},{8,16},{16,8},{24,0},{1,25},{9,17},{17,9},{25,1},{2,26},{10... | collective-permute-start | bytes 393224 | tf_op jit(solution)/shard_map/ppermute | solution.py:56
  714.7 27.5 %collective-permute-start.37 = (bf16[4,2,64,768]{3,2,1,0:T(8,128)(2,1)S(1)}, bf16[4,2,64,768]{3,2,1,0:T(8,128)(2,1)S(1)}, u32[]{:S(2)}, u32[]{:S(2)}) collective-permute-start(bf16[4,2,64,768]{3,2,1,0:T(8,128)(2,1)S(1)} %fusion.101), channel_id=1, source_target_pairs={{0,2},{1,3},{2,0},{3,1},{4,6},{5,7},{6,4},{7,5},{8,10},{9,11},{10,... | collective-permute-start | bytes 2359304 | tf_op jit(solution)/shard_map/ppermute | solution.py:56
  725.5 25.2 %collective-permute-start.52 = (bf16[64,1024]{1,0:T(8,128)(2,1)}, bf16[64,1024]{1,0:T(8,128)(2,1)S(1)}, u32[]{:S(2)}, u32[]{:S(2)}) collective-permute-start(bf16[64,1024]{1,0:T(8,128)(2,1)} %get-tuple-element.382), channel_id=1, source_target_pairs={{0,24},{8,16},{16,8},{24,0},{1,25},{9,17},{17,9},{25,1},{2,26},{10... | collective-permute-start | bytes 393224 | tf_op jit(solution)/shard_map/ppermute | solution.py:56
  742.2 24.3 %collective-permute-start.44 = (bf16[1,1,64,2048]{3,2,1,0:T(8,128)(2,1)}, bf16[1,1,64,2048]{3,2,1,0:T(8,128)(2,1)S(1)}, u32[]{:S(2)}, u32[]{:S(2)}) collective-permute-start(bf16[1,1,64,2048]{3,2,1,0:T(8,128)(2,1)} %dynamic-slice_convert_fusion.5), channel_id=1, source_target_pairs={{0,4},{1,5},{2,6},{3,7},{4,0},{5,1},{6,2},{7,3},{8,12},{9,13},{10,... | collective-permute-start | bytes 786440 | tf_op jit(solution)/shard_map/ppermute | solution.py:56
  744.8 29.2 %collective-permute-start.38 = (bf16[4,1,64,768]{3,2,1,0:T(8,128)(2,1)S(1)}, bf16[4,1,64,768]{3,2,1,0:T(8,128)(2,1)}, u32[]{:S(2)}, u32[]{:S(2)}) collective-permute-start(bf16[4,1,64,768]{3,2,1,0:T(8,128)(2,1)S(1)} %dynamic-slice_convert_fusion.4), channel_id=1, source_target_pairs={{0,4},{1,5},{2,6},{3,7},{4,0},{5,1},{6,2},{7,3},{8,12},{9,13},{10,... | collective-permute-start | bytes 1179656 | tf_op jit(solution)/shard_map/ppermute | solution.py:56
  748.8 75.6 %collective-permute-start.31 = (bf16[256,2048]{1,0:T(8,128)(2,1)}, bf16[256,2048]{1,0:T(8,128)(2,1)}, u32[]{:S(2)}, u32[]{:S(2)}) collective-permute-start(bf16[256,2048]{1,0:T(8,128)(2,1)} %slice.274), channel_id=1, source_target_pairs={{0,16},{8,24},{16,0},{24,8},{1,17},{9,25},{17,1},{25,9},{2,18},{10... | collective-permute-start | bytes 3145736 | tf_op jit(solution)/shard_map/ppermute | solution.py:56
  783.5 52.0 %collective-permute-start.35 = (bf16[256,2048]{1,0:T(8,128)(2,1)}, bf16[256,2048]{1,0:T(8,128)(2,1)}, u32[]{:S(2)}, u32[]{:S(2)}) collective-permute-start(bf16[256,2048]{1,0:T(8,128)(2,1)} %slice.273), channel_id=1, source_target_pairs={{0,16},{8,24},{16,0},{24,8},{1,17},{9,25},{17,1},{25,9},{2,18},{10... | collective-permute-start | bytes 3145736 | tf_op jit(solution)/shard_map/ppermute | solution.py:56
  783.8 30.3 %collective-permute-start.40 = (f32[64,768]{1,0:T(8,128)}, f32[64,768]{1,0:T(8,128)}, u32[]{:S(2)}, u32[]{:S(2)}) collective-permute-start(f32[64,768]{1,0:T(8,128)} %get-tuple-element.379), channel_id=1, source_target_pairs={{0,16},{8,24},{16,0},{24,8},{1,17},{9,25},{17,1},{25,9},{2,18},{10... | collective-permute-start | bytes 589832 | tf_op jit(solution)/shard_map/ppermute | solution.py:56
  785.6 31.7 %collective-permute-start.41 = (f32[64,768]{1,0:T(8,128)}, f32[64,768]{1,0:T(8,128)}, u32[]{:S(2)}, u32[]{:S(2)}) collective-permute-start(f32[64,768]{1,0:T(8,128)} %get-tuple-element.378), channel_id=1, source_target_pairs={{0,24},{8,16},{16,8},{24,0},{1,25},{9,17},{17,9},{25,1},{2,26},{10... | collective-permute-start | bytes 589832 | tf_op jit(solution)/shard_map/ppermute | solution.py:56
  (141 other events, 2224.6 us)
Sparse Core Ops, SparseCore 0:
  31.0 62.0 all-gather.2
  137.0 203.5 all-gather.4
  420.3 43.6 reduce-scatter.8
  466.2 42.8 reduce-scatter.10
  525.7 43.5 reduce-scatter.4
  572.1 42.8 reduce-scatter.6
where the time goes:
time: 902 us; the launch traced here: 891 us
  waiting for transfers between devices  406 us (45%)
  matrix products  178 us (20%)
  other arithmetic  102 us (11%)
  local copies, waits for them, and re-layouts  78.2 us (9%)
  starting transfers between devices  71 us (8%)
  between operations  29.3 us (3%)
  Pallas kernels  17.8 us (2%)
    ppermute x70, waiting for transfers between devices, swap(): return lax.ppermute(value, axis, [(i, i ^ distance) for i in range(count)])  395 us
    ppermute x70, starting transfers between devices, swap(): return lax.ppermute(value, axis, [(i, i ^ distance) for i in range(count)])  70.4 us
    dot_general x6, matrix products, times_transpose(): lax.dot_general(left_side, right_side, (((1,), (1,)), ((), ())), preferre...  54.2 us
    dot_general x6, matrix products, product(): return jnp.dot(left_side, right_side, preferred_element_type=jnp.float32)  46.5 us
    dot_general x6, matrix products, column_product(): lax.dot_general(left_side, right_side, (((0,), (0,)), ((), ())), preferre...  34.1 us
    unnamed x198, local copies, waits for them, and re-layouts  22.6 us
  transfers between devices with their start and end apart: 76, of which 28 were waited for; matrix products, arithmetic and copies ran while one was open for 37% of the time, Pallas kernels for 0%

commit v1 on v0

--- a/solution.py
+++ b/solution.py
@@ -374,12 +374,12 @@
     ln_one_own = layer_norm(hidden, affine_master[0], affine_master[1]).astype(low)
     ln_one = gather_tokens(ln_one_own, count)
     mixed = product(ln_one, mixer_w).astype(low)
-    mixed, reduce_rows = lax.optimization_barrier((mixed, late_reduce.astype(low)))
-    reduce_w = lax.all_gather(reduce_rows, "fsdp", axis=0, tiled=True)
     queries = mixed[:, :width].reshape(group_tokens, heads, HEAD)
     key_rows = mixed[:, width : width + HEAD]
     value_rows = mixed[:, width + HEAD :]
     head_out, logsum = attend_forward(queries, key_rows, value_rows, places, segments)
+    head_out, reduce_rows = lax.optimization_barrier((head_out, late_reduce.astype(low)))
+    reduce_w = lax.all_gather(reduce_rows, "fsdp", axis=0, tiled=True)
     attended = head_out.reshape(group_tokens, width)
 
     def project_rows(start, stop):
@@ -393,10 +393,12 @@
     expanded = product(ln_two, expand_w)
     activated = activate(expanded).astype(low)
 
+    squares = []
     reduce_halves = []
     for h in range(2):
         part = column_product(activated, cotangent[:, h * D // 2 : (h + 1) * D // 2])
         reduce_halves.append(scatter_mixed(part[None], shard, shards)[0])
+        squares.append(jnp.sum(jnp.square(reduce_halves[h].astype(jnp.float32))))
     grad_activated = times_transpose(cotangent, reduce_w)
     _, gelu_pull = jax.vjp(activate, expanded)
     grad_expanded = gelu_pull(grad_activated)[0].astype(low)
@@ -409,6 +411,7 @@
     for h in range(2):
         part = column_product(ln_two, grad_expanded[:, h * slab // 2 : (h + 1) * slab // 2])
         part = scatter_mixed(part.reshape(count, D // count, slab // 2), shard, shards)
+        squares.append(jnp.sum(jnp.square(part.astype(jnp.float32))))
         expand_halves.append(trade(lambda m: part[m], member, count))
     expand_pieces = list(zip(*expand_halves))
 
@@ -439,6 +442,7 @@
     )
     mixer_part = column_product(ln_one, grad_mixed)
     mixer_part = scatter_rows(mixer_part.reshape(count, D // count, width + KV), shard, shards)
+    squares.append(jnp.sum(jnp.square(mixer_part[:, :, :width])))
     mixer_pieces = trade(lambda m: mixer_part[m], member, count)
 
     def first_rows(start, stop):
@@ -450,17 +454,10 @@
     input_grad = (grad_middle + grad_hidden).astype(low)[None]
 
     affine_grad = butterfly(jnp.stack([gain_one, shift_one, gain_two, shift_two]), counts)
-    expand_squares = [
-        jnp.sum(jnp.square(p.astype(jnp.float32))) for ps in [*expand_pieces, reduce_halves] for p in ps
-    ]
-    mixer_squares = [jnp.sum(jnp.square(p[:, :width])) for p in mixer_pieces]
     shared_grad = sum(p[:, width:] for p in mixer_pieces)
-    local_square = (
-        sum(mixer_squares)
-        + jnp.sum(shared_grad * shared_grad)
-        + jnp.sum(project_grad * project_grad)
-        + sum(expand_squares)
-    )
+    squares.append(jnp.sum(shared_grad * shared_grad))
+    squares.append(jnp.sum(project_grad * project_grad))
+    local_square = sum(squares)
     square_total = total_over_mesh(local_square, member * shards + shard, counts) + jnp.sum(
         affine_grad * affine_grad
     )

time: 902 us -> 860 us (0.953)
  waiting for transfers between devices: 406 us -> 384 us
  other arithmetic: 102 us -> 91.1 us
    ppermute x70, waiting for transfers between devices: 395 us -> 372 us  [swap(): return lax.ppermute(value, axis, [(i, i ^ distance) for i in range(count)])]
    reduce_sum x16 -> x7, other arithmetic: 18.8 us -> 10.6 us  [the longest x2 3.83 us: local_step(): squares.append(jnp.sum(jnp.square(part.astype(jnp.float32))))]
    unnamed x198 -> x189, local copies, waits for them, and re-layouts: 22.6 us -> 27 us
  transfers between devices with their start and end apart: 76 -> 76, of which waited for: 28 -> 27; matrix products, arithmetic and copies ran while one was open for 37% -> 37% of each run, Pallas kernels for 0% -> 1%
where the time goes in v1:
time: 860 us; the launch traced here: 853 us
  waiting for transfers between devices  384 us (45%)
  matrix products  173 us (20%)
  other arithmetic  91.1 us (11%)
  local copies, waits for them, and re-layouts  80.7 us (9%)
  starting transfers between devices  74.7 us (9%)
  between operations  23.4 us (3%)
  Pallas kernels  17.6 us (2%)
    ppermute x70, waiting for transfers between devices, swap(): return lax.ppermute(value, axis, [(i, i ^ distance) for i in range(count)])  372 us
    ppermute x70, starting transfers between devices, swap(): return lax.ppermute(value, axis, [(i, i ^ distance) for i in range(count)])  74.2 us
    dot_general x6, matrix products, times_transpose(): lax.dot_general(left_side, right_side, (((1,), (1,)), ((), ())), preferre...  49.8 us
    dot_general x6, matrix products, product(): return jnp.dot(left_side, right_side, preferred_element_type=jnp.float32)  46.3 us
    dot_general x6, matrix products, column_product(): lax.dot_general(left_side, right_side, (((0,), (0,)), ((), ())), preferre...  33.9 us
    unnamed x189, local copies, waits for them, and re-layouts  27 us
    pallas_call x3, Pallas kernels, fold_update(): pl.pallas_call(functools.partial(fold_kernel, count, widths, extra), out_...  17.6 us
    convert_element_type x4, other arithmetic, scatter_mixed(): kept = kept.astype(low)  17.5 us
  transfers between devices with their start and end apart: 76, of which 27 were waited for; matrix products, arithmetic and copies ran while one was open for 37% of the time, Pallas kernels for 1%

profile of v1, /device:TPU:0, one launch (start us, length us, event | category | flops | bytes accessed | tf_op | source)
XLA Modules:
  0.0 853.1 jit_solution(2702970635230175089)
XLA Ops:
  43.1 11.9 %collective-permute-done.12 = bf16[1,64,2048]{2,1,0:T(8,128)(2,1)S(1)} collective-permute-done((bf16[1,64,2048]{2,1,0:T(8,128)(2,1)}, bf16[1,64,2048]{2,1,0:T(8,128)(2,1)S(1)}, u32[]{:S(2)}, u32[]{:S(2)}) %collective-permute-start.12) | collective-permute-done | bytes 262176 | tf_op jit(solution)/shard_map/ppermute | solution.py:56
  56.5 16.7 %collective-permute-done.5 = bf16[256,2048]{1,0:T(8,128)(2,1)} collective-permute-done((bf16[256,2048]{1,0:T(8,128)(2,1)}, bf16[256,2048]{1,0:T(8,128)(2,1)}, u32[]{:S(2)}, u32[]{:S(2)}) %collective-permute-start.5) | collective-permute-done | bytes 1048608 | tf_op jit(solution)/shard_map/ppermute | solution.py:56
  79.3 11.7 %all-gather.3.cloned.1.call-done = bf16[4,512,768]{2,1,0:T(8,128)(2,1)} async-done(((bf16[4,64,768]{2,1,0:T(8,128)(2,1)}), bf16[4,512,768]{2,1,0:T(8,128)(2,1)}) %all-gather.3.cloned.1.call-update) | async-done | bytes 3145744 | tf_op jit(solution)/shard_map/all_gather | solution.py:369
  91.1 6.6 fusion.95
  101.0 23.9 %while.27 = (s32[]{:T(128)}, bf16[2,512,4,128]{3,1,0,2:T(8,128)(2,1)}, f32[2,4,512]{2,1,0:T(4,128)}, s32[1024]{0:T(1024)S(1)}, s32[2]{0:T(128)S(1)}, /*index=5*/...) while((s32[]{:T(128)}, ...), condition=%wide.region_5.6_spmd, body=%wide.region_2.5_spmd.sunk | while | flops 1101790720 | bytes 37317876 | solution.py:197
  128.5 4.4 convolution_convert_fusion.3
  141.4 4.2 collective-permute-done.19
  168.3 58.2 %collective-permute-done.24 = bf16[4,64,2048]{2,1,0:T(8,128)(2,1)} collective-permute-done((bf16[4,64,2048]{2,1,0:T(8,128)(2,1)}, bf16[4,64,2048]{2,1,0:T(8,128)(2,1)}, u32[]{:S(2)}, u32[]{:S(2)}) %collective-permute-start.24) | collective-permute-done | bytes 1048608 | tf_op jit(solution)/shard_map/ppermute | solution.py:56
  228.4 4.1 collective-permute-start.26
  239.5 50.1 %collective-permute-done.26 = bf16[4,64,2048]{2,1,0:T(8,128)(2,1)S(1)} collective-permute-done((bf16[4,64,2048]{2,1,0:T(8,128)(2,1)}, bf16[4,64,2048]{2,1,0:T(8,128)(2,1)S(1)}, u32[]{:S(2)}, u32[]{:S(2)}) %collective-permute-start.26) | collective-permute-done | bytes 1048608 | tf_op jit(solution)/shard_map/ppermute | solution.py:56
  291.1 26.2 %collective-permute-done.23 = bf16[4,64,2048]{2,1,0:T(8,128)(2,1)S(1)} collective-permute-done((bf16[4,64,2048]{2,1,0:T(8,128)(2,1)}, bf16[4,64,2048]{2,1,0:T(8,128)(2,1)S(1)}, u32[]{:S(2)}, u32[]{:S(2)}) %collective-permute-start.23) | collective-permute-done | bytes 1048608 | tf_op jit(solution)/shard_map/ppermute | solution.py:56
  322.3 17.4 %collective-permute-done.27 = bf16[4,64,2048]{2,1,0:T(8,128)(2,1)S(1)} collective-permute-done((bf16[4,64,2048]{2,1,0:T(8,128)(2,1)S(1)}, bf16[4,64,2048]{2,1,0:T(8,128)(2,1)S(1)}, u32[]{:S(2)}, u32[]{:S(2)}) %collective-permute-start.27) | collective-permute-done | bytes 1048608 | tf_op jit(solution)/shard_map/ppermute | solution.py:56
  339.8 4.0 copy-done.95
  343.8 14.1 %multiply_convert_fusion = (bf16[1024,2048]{1,0:T(8,128)(2,1)S(1)}, f32[1024,2048]{1,0:T(8,128)}) fusion(bf16[2048,2048]{1,0:T(8,128)(2,1)S(1)} %bitcast.405, bf16[512,2048]{1,0:T(8,128)(2,1)} %copy-done.95, bf16[256,2048]{1,0:T(8,128)(2,1)S(1)} %copy-done.60, bf16[256,2048]{1,0:T(8,128)(2,1)S(1)} %add_convert_fusion.1), kind=kOutput, calls=%fused_computation.68 | convolution fusion | flops 8621391872 | bytes 25165824 | tf_op jit(solution)/shard_map/dot_general | solution.py:40
  358.0 4.7 fusion.82
  368.0 7.2 fusion.80
  381.7 34.7 %collective-permute-done.36 = bf16[1,4,256,1024]{3,2,1,0:T(8,128)(2,1)} collective-permute-done((bf16[1,4,256,1024]{3,2,1,0:T(8,128)(2,1)}, bf16[1,4,256,1024]{3,2,1,0:T(8,128)(2,1)}, u32[]{:S(2)}, u32[]{:S(2)}) %collective-permute-start.36) | collective-permute-done | bytes 2097184 | tf_op jit(solution)/shard_map/ppermute | solution.py:56
  420.3 20.7 %fusion.52 = bf16[1024,2048]{1,0:T(8,128)(2,1)} fusion(f32[1024,2048]{1,0:T(8,128)} %get-tuple-element.403, bf16[2048,2048]{1,0:T(8,128)(2,1)} %all-gather.5.cloned.1.call-done, bf16[512,2048]{1,0:T(8,128)(2,1)} %copy-done.47, bf16[256,2048]{1,0:T(8,128)(2,1)} %collective-permute-done, bf16[256,2048]{1,0:T(8,128)(2,1)S(1)} %bitcast.399), kind=kOutput, calls=%fused_computation.67 | convolution fusion | flops 8644460544 | bytes 25165824 | tf_op jit(solution)/shard_map/dot_general | solution.py:44
  440.9 9.9 %convolution_convert_fusion.2 = bf16[512,2048]{1,0:T(8,128)(2,1)} fusion(bf16[2048,2048]{1,0:T(8,128)(2,1)} %bitcast.406, bf16[1024,2048]{1,0:T(8,128)(2,1)} %fusion.52), kind=kOutput, calls=%fused_computation.96 | convolution fusion | flops 4296015872 | bytes 12582912 | tf_op jit(solution)/shard_map/dot_general | solution.py:44
  450.9 9.4 %collective-permute-done.37 = bf16[1,4,256,1024]{3,2,1,0:T(8,128)(2,1)} collective-permute-done((bf16[1,4,256,1024]{3,2,1,0:T(8,128)(2,1)}, bf16[1,4,256,1024]{3,2,1,0:T(8,128)(2,1)}, u32[]{:S(2)}, u32[]{:S(2)}) %collective-permute-start.37) | collective-permute-done | bytes 2097184 | tf_op jit(solution)/shard_map/ppermute | solution.py:56
  460.3 5.0 fusion.57
  465.3 7.4 fusion.78
  473.5 9.3 %convert_add_fusion.2 = f32[512,2048]{1,0:T(8,128)S(1)} fusion(bf16[512,2048]{1,0:T(8,128)(2,1)} %collective-permute-done.28, bf16[2048,2048]{1,0:T(8,128)(2,1)} %bitcast.407, bf16[1024,2048]{1,0:T(8,128)(2,1)} %fusion.52), kind=kOutput, calls=%fused_computation.88 | convolution fusion | flops 4297064448 | bytes 16777216 | tf_op jit(solution)/shard_map/dot_general | solution.py:44
  485.6 7.0 fusion.76
  496.0 25.8 %collective-permute-done.38 = bf16[4,4,64,1024]{3,2,1,0:T(8,128)(2,1)} collective-permute-done((bf16[4,4,64,1024]{3,2,1,0:T(8,128)(2,1)S(1)}, bf16[4,4,64,1024]{3,2,1,0:T(8,128)(2,1)}, u32[]{:S(2)}, u32[]{:S(2)}) %collective-permute-start.38) | collective-permute-done | bytes 2097184 | tf_op jit(solution)/shard_map/ppermute | solution.py:56
  521.7 3.8 fusion.56
  533.1 9.5 %convolution_convert_fusion.1 = bf16[512,2048]{1,0:T(8,128)(2,1)} fusion(bf16[2048,2048]{1,0:T(8,128)(2,1)} %all-gather.5.cloned.1.call-done, bf16[1024,2048]{1,0:T(8,128)(2,1)S(1)} %copy-done.99), kind=kOutput, calls=%fused_computation.95 | convolution fusion | flops 4296015872 | bytes 12582912 | tf_op jit(solution)/shard_map/dot_general | solution.py:40
  550.5 14.2 %collective-permute-done.39 = bf16[4,4,64,1024]{3,2,1,0:T(8,128)(2,1)} collective-permute-done((bf16[4,4,64,1024]{3,2,1,0:T(8,128)(2,1)}, bf16[4,4,64,1024]{3,2,1,0:T(8,128)(2,1)}, u32[]{:S(2)}, u32[]{:S(2)}) %collective-permute-start.39) | collective-permute-done | bytes 2097184 | tf_op jit(solution)/shard_map/ppermute | solution.py:56
  564.7 5.0 fusion.55
  572.8 8.6 %convert_add_fusion.1 = f32[512,2048]{1,0:T(8,128)S(1)} fusion(bf16[512,2048]{1,0:T(8,128)(2,1)} %collective-permute-done.30, bf16[2048,2048]{1,0:T(8,128)(2,1)} %all-gather.5.cloned.1.call-done, bf16[1024,2048]{1,0:T(8,128)(2,1)S(1)} %copy-done.100), kind=kOutput, calls=%fused_computation.87 | convolution fusion | flops 4297064448 | bytes 16777216 | tf_op jit(solution)/shard_map/dot_general | solution.py:40
  588.1 50.6 %while.28 = (s32[]{:T(128)}, f32[1024,128]{1,0:T(8,128)S(1)}, f32[1024,128]{1,0:T(8,128)S(1)}, bf16[2,512,4,128]{3,2,1,0:T(4,128)(2,1)}, s32[1024]{0:T(1024)S(1)...) while((s32[]{:T(128)}, f32[1024,128]{1,0:T(8,128)S(1)}, ...), condition=%wide.region_12.13_spmd.clone, body=%wide.region_10.12_spmd.clone.sunk | while | flops 2719612416 | bytes 138759600 | solution.py:234
  592.9 4.0 fusion.184
  596.9 3.7 fusion.185
  600.6 3.7 fusion.186
  604.3 6.4 fusion.187
  618.0 4.0 fusion.184
  622.0 3.7 fusion.185
  629.4 6.3 fusion.187
  649.5 5.4 fusion.93
  669.6 6.0 collective-permute-done.46
  678.8 30.1 %collective-permute-done.40 = bf16[4,4,64,768]{3,2,1,0:T(8,128)(2,1)} collective-permute-done((bf16[4,4,64,768]{3,2,1,0:T(8,128)(2,1)}, bf16[4,4,64,768]{3,2,1,0:T(8,128)(2,1)}, u32[]{:S(2)}, u32[]{:S(2)}) %collective-permute-start.40) | collective-permute-done | bytes 1572896 | tf_op jit(solution)/shard_map/ppermute | solution.py:56
  716.5 19.9 %collective-permute-done.41 = bf16[4,2,64,768]{3,2,1,0:T(8,128)(2,1)S(1)} collective-permute-done((bf16[4,2,64,768]{3,2,1,0:T(8,128)(2,1)S(1)}, bf16[4,2,64,768]{3,2,1,0:T(8,128)(2,1)S(1)}, u32[]{:S(2)}, u32[]{:S(2)}) %collective-permute-start.41) | collective-permute-done | bytes 786464 | tf_op jit(solution)/shard_map/ppermute | solution.py:56
  746.1 9.7 %collective-permute-done.42 = bf16[4,1,64,768]{3,2,1,0:T(8,128)(2,1)S(1)} collective-permute-done((bf16[4,1,64,768]{3,2,1,0:T(8,128)(2,1)S(1)}, bf16[4,1,64,768]{3,2,1,0:T(8,128)(2,1)S(1)}, u32[]{:S(2)}, u32[]{:S(2)}) %collective-permute-start.42) | collective-permute-done | bytes 393248 | tf_op jit(solution)/shard_map/ppermute | solution.py:56
  761.4 12.3 %collective-permute-done.45.refs_3_ = f32[64,768]{1,0:T(8,128)S(1)} collective-permute-done((f32[64,768]{1,0:T(8,128)}, f32[64,768]{1,0:T(8,128)S(1)}, u32[]{:S(2)}, u32[]{:S(2)}) %collective-permute-start.45) | collective-permute-done | bytes 196640 | tf_op jit(solution)/shard_map/ppermute | solution.py:56
  802.9 4.3 collective-permute-done.60
  826.4 6.8 fold_update.5
  833.2 4.1 fold_update.3
  838.0 6.8 fold_update.4
  (534 shorter events, 272.4 us)
Async XLA Ops:
  7.2 83.9 %all-gather.3.cloned.1.call-start = ((), (), s32[]{:S(2)}) async-start(), calls=%async_computation.4 | async-start | bytes 3538944 | tf_op jit(solution)/shard_map/all_gather | solution.py:369
  9.1 30.1 %collective-permute-start.7 = (bf16[1,64,2048]{2,1,0:T(8,128)(2,1)}, bf16[1,64,2048]{2,1,0:T(8,128)(2,1)}, u32[]{:S(2)}, u32[]{:S(2)}) collective-permute-start(bf16[1,64,2048]{2,1,0:T(8,128)(2,1)} %convert_bitcast_fusion.1), channel_id=1, source_target_pairs={{0,1},{1,0},{2,3},{3,2},{4,5},{5,4},{6,7},{7,6},{8,9},{9,8},{10,11... | collective-permute-start | bytes 786440 | tf_op jit(solution)/shard_map/ppermute | solution.py:56
  12.1 27.6 %collective-permute-start.8 = (bf16[1,64,2048]{2,1,0:T(8,128)(2,1)}, bf16[1,64,2048]{2,1,0:T(8,128)(2,1)}, u32[]{:S(2)}, u32[]{:S(2)}) collective-permute-start(bf16[1,64,2048]{2,1,0:T(8,128)(2,1)} %convert_bitcast_fusion.1), channel_id=1, source_target_pairs={{0,2},{1,3},{2,0},{3,1},{4,6},{5,7},{6,4},{7,5},{8,10},{9,11},{10,... | collective-permute-start | bytes 786440 | tf_op jit(solution)/shard_map/ppermute | solution.py:56
  13.7 24.9 %collective-permute-start.10 = (bf16[1,64,2048]{2,1,0:T(8,128)(2,1)}, bf16[1,64,2048]{2,1,0:T(8,128)(2,1)}, u32[]{:S(2)}, u32[]{:S(2)}) collective-permute-start(bf16[1,64,2048]{2,1,0:T(8,128)(2,1)} %convert_bitcast_fusion.1), channel_id=1, source_target_pairs={{0,4},{1,5},{2,6},{3,7},{4,0},{5,1},{6,2},{7,3},{8,12},{9,13},{10,... | collective-permute-start | bytes 786440 | tf_op jit(solution)/shard_map/ppermute | solution.py:56
  23.3 143.2 %collective-permute-start = (bf16[256,2048]{1,0:T(8,128)(2,1)}, bf16[256,2048]{1,0:T(8,128)(2,1)}, u32[]{:S(2)}, u32[]{:S(2)}) collective-permute-start(bf16[256,2048]{1,0:T(8,128)(2,1)} %bitcast.396), channel_id=1, source_target_pairs={{0,16},{8,24},{16,0},{24,8},{1,17},{9,25},{17,1},{25,9},{2,18},{10... | collective-permute-start | bytes 3145736 | tf_op jit(solution)/shard_map/ppermute | solution.py:56
  28.6 391.7 %all-gather.5.cloned.1.call-start = ((), (), s32[]{:S(2)}) async-start(), calls=%async_computation.5 | async-start | bytes 9437184 | tf_op jit(solution)/shard_map/all_gather | solution.py:382
  32.0 41.1 %collective-permute-start.5 = (bf16[256,2048]{1,0:T(8,128)(2,1)}, bf16[256,2048]{1,0:T(8,128)(2,1)}, u32[]{:S(2)}, u32[]{:S(2)}) collective-permute-start(bf16[256,2048]{1,0:T(8,128)(2,1)} %fusion.68), channel_id=1, source_target_pairs={{0,16},{8,24},{16,0},{24,8},{1,17},{9,25},{17,1},{25,9},{2,18},{10... | collective-permute-start | bytes 3145736 | tf_op jit(solution)/shard_map/ppermute | solution.py:56
  38.6 37.5 %collective-permute-start.11 = (bf16[1,64,2048]{2,1,0:T(8,128)(2,1)}, bf16[1,64,2048]{2,1,0:T(8,128)(2,1)S(1)}, u32[]{:S(2)}, u32[]{:S(2)}) collective-permute-start(bf16[1,64,2048]{2,1,0:T(8,128)(2,1)} %collective-permute-done.10), channel_id=1, source_target_pairs={{0,1},{1,0},{2,3},{3,2},{4,5},{5,4},{6,7},{7,6},{8,9},{9,8},{10,11... | collective-permute-start | bytes 786440 | tf_op jit(solution)/shard_map/ppermute | solution.py:56
  39.7 35.3 %collective-permute-start.9 = (bf16[1,64,2048]{2,1,0:T(8,128)(2,1)}, bf16[1,64,2048]{2,1,0:T(8,128)(2,1)S(1)}, u32[]{:S(2)}, u32[]{:S(2)}) collective-permute-start(bf16[1,64,2048]{2,1,0:T(8,128)(2,1)} %collective-permute-done.8), channel_id=1, source_target_pairs={{0,1},{1,0},{2,3},{3,2},{4,5},{5,4},{6,7},{7,6},{8,9},{9,8},{10,11... | collective-permute-start | bytes 786440 | tf_op jit(solution)/shard_map/ppermute | solution.py:56
  55.0 21.1 %collective-permute-start.13 = (bf16[1,64,2048]{2,1,0:T(8,128)(2,1)S(1)}, bf16[1,64,2048]{2,1,0:T(8,128)(2,1)S(1)}, u32[]{:S(2)}, u32[]{:S(2)}) collective-permute-start(bf16[1,64,2048]{2,1,0:T(8,128)(2,1)S(1)} %collective-permute-done.12), channel_id=1, source_target_pairs={{0,1},{1,0},{2,3},{3,2},{4,5},{5,4},{6,7},{7,6},{8,9},{9,8},{10,11... | collective-permute-start | bytes 786440 | tf_op jit(solution)/shard_map/ppermute | solution.py:56
  132.9 22.7 %collective-permute-start.14 = (bf16[512,2048]{1,0:T(8,128)(2,1)}, bf16[512,2048]{1,0:T(8,128)(2,1)}, u32[]{:S(2)}, u32[]{:S(2)}) collective-permute-start(bf16[512,2048]{1,0:T(8,128)(2,1)} %convolution_convert_fusion.3), channel_id=1, source_target_pairs={{0,8},{8,0},{16,24},{24,16},{1,9},{9,1},{17,25},{25,17},{2,10},{10... | collective-permute-start | bytes 6291464 | tf_op jit(solution)/shard_map/ppermute | solution.py:56
  137.6 407.8 %reduce-scatter.5.cloned.1.call-start = ((), (), s32[]{:S(2)}) async-start(), calls=%async_computation.6 | async-start | bytes 2621440 | tf_op jit(solution)/shard_map/reduce_scatter | solution.py:123
  151.0 77.3 %collective-permute-start.22 = (bf16[4,64,2048]{2,1,0:T(8,128)(2,1)}, bf16[4,64,2048]{2,1,0:T(8,128)(2,1)}, u32[]{:S(2)}, u32[]{:S(2)}) collective-permute-start(bf16[4,64,2048]{2,1,0:T(8,128)(2,1)} %bitcast_dynamic-update-slice_fusion.9), channel_id=1, source_target_pairs={{0,2},{1,3},{2,0},{3,1},{4,6},{5,7},{6,4},{7,5},{8,10},{9,11},{10,... | collective-permute-start | bytes 3145736 | tf_op jit(solution)/shard_map/ppermute | solution.py:56
  152.5 74.0 %collective-permute-start.24 = (bf16[4,64,2048]{2,1,0:T(8,128)(2,1)}, bf16[4,64,2048]{2,1,0:T(8,128)(2,1)}, u32[]{:S(2)}, u32[]{:S(2)}) collective-permute-start(bf16[4,64,2048]{2,1,0:T(8,128)(2,1)} %bitcast_dynamic-update-slice_fusion.9), channel_id=1, source_target_pairs={{0,4},{1,5},{2,6},{3,7},{4,0},{5,1},{6,2},{7,3},{8,12},{9,13},{10,... | collective-permute-start | bytes 3145736 | tf_op jit(solution)/shard_map/ppermute | solution.py:56
  160.9 71.5 %collective-permute-start.15 = (bf16[256,2048]{1,0:T(8,128)(2,1)S(1)}, bf16[256,2048]{1,0:T(8,128)(2,1)S(1)}, u32[]{:S(2)}, u32[]{:S(2)}) collective-permute-start(bf16[256,2048]{1,0:T(8,128)(2,1)S(1)} %slice.252), channel_id=1, source_target_pairs={{0,16},{8,24},{16,0},{24,8},{1,17},{9,25},{17,1},{25,9},{2,18},{10... | collective-permute-start | bytes 3145736 | tf_op jit(solution)/shard_map/ppermute | solution.py:56
  162.5 74.0 %collective-permute-start.21 = (bf16[4,64,2048]{2,1,0:T(8,128)(2,1)}, bf16[4,64,2048]{2,1,0:T(8,128)(2,1)S(1)}, u32[]{:S(2)}, u32[]{:S(2)}) collective-permute-start(bf16[4,64,2048]{2,1,0:T(8,128)(2,1)} %bitcast_dynamic-update-slice_fusion.9), channel_id=1, source_target_pairs={{0,1},{1,0},{2,3},{3,2},{4,5},{5,4},{6,7},{7,6},{8,9},{9,8},{10,11... | collective-permute-start | bytes 3145736 | tf_op jit(solution)/shard_map/ppermute | solution.py:56
  168.0 151.6 %collective-permute-start.1 = (bf16[512,2048]{1,0:T(8,128)(2,1)S(1)}, bf16[512,2048]{1,0:T(8,128)(2,1)S(1)}, u32[]{:S(2)}, u32[]{:S(2)}) collective-permute-start(bf16[512,2048]{1,0:T(8,128)(2,1)S(1)} %pad_maximum_fusion.3), channel_id=1, source_target_pairs={{0,8},{8,0},{16,24},{24,16},{1,9},{9,1},{17,25},{25,17},{2,10},{10... | collective-permute-start | bytes 6291464 | tf_op jit(solution)/shard_map/ppermute | solution.py:56
  226.5 92.7 %collective-permute-start.25 = (bf16[4,64,2048]{2,1,0:T(8,128)(2,1)}, bf16[4,64,2048]{2,1,0:T(8,128)(2,1)S(1)}, u32[]{:S(2)}, u32[]{:S(2)}) collective-permute-start(bf16[4,64,2048]{2,1,0:T(8,128)(2,1)} %collective-permute-done.24), channel_id=1, source_target_pairs={{0,1},{1,0},{2,3},{3,2},{4,5},{5,4},{6,7},{7,6},{8,9},{9,8},{10,11... | collective-permute-start | bytes 3145736 | tf_op jit(solution)/shard_map/ppermute | solution.py:56
  228.4 61.2 %collective-permute-start.26 = (bf16[4,64,2048]{2,1,0:T(8,128)(2,1)}, bf16[4,64,2048]{2,1,0:T(8,128)(2,1)S(1)}, u32[]{:S(2)}, u32[]{:S(2)}) collective-permute-start(bf16[4,64,2048]{2,1,0:T(8,128)(2,1)} %collective-permute-done.24), channel_id=1, source_target_pairs={{0,2},{1,3},{2,0},{3,1},{4,6},{5,7},{6,4},{7,5},{8,10},{9,11},{10,... | collective-permute-start | bytes 3145736 | tf_op jit(solution)/shard_map/ppermute | solution.py:56
  233.4 84.0 %collective-permute-start.23 = (bf16[4,64,2048]{2,1,0:T(8,128)(2,1)}, bf16[4,64,2048]{2,1,0:T(8,128)(2,1)S(1)}, u32[]{:S(2)}, u32[]{:S(2)}) collective-permute-start(bf16[4,64,2048]{2,1,0:T(8,128)(2,1)} %collective-permute-done.22), channel_id=1, source_target_pairs={{0,1},{1,0},{2,3},{3,2},{4,5},{5,4},{6,7},{7,6},{8,9},{9,8},{10,11... | collective-permute-start | bytes 3145736 | tf_op jit(solution)/shard_map/ppermute | solution.py:56
  236.5 81.0 %collective-permute-start.16 = (bf16[256,2048]{1,0:T(8,128)(2,1)S(1)}, bf16[256,2048]{1,0:T(8,128)(2,1)S(1)}, u32[]{:S(2)}, u32[]{:S(2)}) collective-permute-start(bf16[256,2048]{1,0:T(8,128)(2,1)S(1)} %add_convert_fusion.1), channel_id=1, source_target_pairs={{0,16},{8,24},{16,0},{24,8},{1,17},{9,25},{17,1},{25,9},{2,18},{10... | collective-permute-start | bytes 3145736 | tf_op jit(solution)/shard_map/ppermute | solution.py:56
  289.6 50.0 %collective-permute-start.27 = (bf16[4,64,2048]{2,1,0:T(8,128)(2,1)S(1)}, bf16[4,64,2048]{2,1,0:T(8,128)(2,1)S(1)}, u32[]{:S(2)}, u32[]{:S(2)}) collective-permute-start(bf16[4,64,2048]{2,1,0:T(8,128)(2,1)S(1)} %collective-permute-done.26), channel_id=1, source_target_pairs={{0,1},{1,0},{2,3},{3,2},{4,5},{5,4},{6,7},{7,6},{8,9},{9,8},{10,11... | collective-permute-start | bytes 3145736 | tf_op jit(solution)/shard_map/ppermute | solution.py:56
  317.7 22.0 %collective-permute-start.17 = (bf16[512,2048]{1,0:T(8,128)(2,1)S(1)}, bf16[512,2048]{1,0:T(8,128)(2,1)S(1)}, u32[]{:S(2)}, u32[]{:S(2)}) collective-permute-start(bf16[512,2048]{1,0:T(8,128)(2,1)S(1)} %pad_maximum_fusion.5), channel_id=1, source_target_pairs={{0,8},{8,0},{16,24},{24,16},{1,9},{9,1},{17,25},{25,17},{2,10},{10... | collective-permute-start | bytes 6291464 | tf_op jit(solution)/shard_map/ppermute | solution.py:56
  367.6 48.8 %collective-permute-start.36 = (bf16[1,4,256,1024]{3,2,1,0:T(8,128)(2,1)}, bf16[1,4,256,1024]{3,2,1,0:T(8,128)(2,1)}, u32[]{:S(2)}, u32[]{:S(2)}) collective-permute-start(bf16[1,4,256,1024]{3,2,1,0:T(8,128)(2,1)} %fusion.74), channel_id=1, source_target_pairs={{0,1},{1,0},{2,3},{3,2},{4,5},{5,4},{6,7},{7,6},{8,9},{9,8},{10,11... | collective-permute-start | bytes 6291464 | tf_op jit(solution)/shard_map/ppermute | solution.py:56
  380.0 80.2 %collective-permute-start.37 = (bf16[1,4,256,1024]{3,2,1,0:T(8,128)(2,1)}, bf16[1,4,256,1024]{3,2,1,0:T(8,128)(2,1)}, u32[]{:S(2)}, u32[]{:S(2)}) collective-permute-start(bf16[1,4,256,1024]{3,2,1,0:T(8,128)(2,1)} %fusion.75), channel_id=1, source_target_pairs={{0,1},{1,0},{2,3},{3,2},{4,5},{5,4},{6,7},{7,6},{8,9},{9,8},{10,11... | collective-permute-start | bytes 6291464 | tf_op jit(solution)/shard_map/ppermute | solution.py:56
  420.2 127.1 %reduce-scatter.7.cloned.1.call-start = ((), (), s32[]{:S(2)}) async-start(), calls=%async_computation.7 | async-start | bytes 2621440 | tf_op jit(solution)/shard_map/reduce_scatter | solution.py:123
  450.9 22.6 %collective-permute-start.28 = (bf16[512,2048]{1,0:T(8,128)(2,1)}, bf16[512,2048]{1,0:T(8,128)(2,1)}, u32[]{:S(2)}, u32[]{:S(2)}) collective-permute-start(bf16[512,2048]{1,0:T(8,128)(2,1)} %convolution_convert_fusion.2), channel_id=1, source_target_pairs={{0,8},{8,0},{16,24},{24,16},{1,9},{9,1},{17,25},{25,17},{2,10},{10... | collective-permute-start | bytes 6291464 | tf_op jit(solution)/shard_map/ppermute | solution.py:56
  465.3 195.6 %reduce-scatter.9.cloned.1.call-start = ((), (), s32[]{:S(2)}) async-start(), calls=%async_computation.8 | async-start | bytes 2621440 | tf_op jit(solution)/shard_map/reduce_scatter | solution.py:123
  473.1 48.7 %collective-permute-start.38 = (bf16[4,4,64,1024]{3,2,1,0:T(8,128)(2,1)S(1)}, bf16[4,4,64,1024]{3,2,1,0:T(8,128)(2,1)}, u32[]{:S(2)}, u32[]{:S(2)}) collective-permute-start(bf16[4,4,64,1024]{3,2,1,0:T(8,128)(2,1)S(1)} %fusion.72), channel_id=1, source_target_pairs={{0,1},{1,0},{2,3},{3,2},{4,5},{5,4},{6,7},{7,6},{8,9},{9,8},{10,11... | collective-permute-start | bytes 6291464 | tf_op jit(solution)/shard_map/ppermute | solution.py:56
  484.1 41.6 %collective-permute-start.29 = (bf16[256,2048]{1,0:T(8,128)(2,1)}, bf16[256,2048]{1,0:T(8,128)(2,1)}, u32[]{:S(2)}, u32[]{:S(2)}) collective-permute-start(bf16[256,2048]{1,0:T(8,128)(2,1)} %slice.251), channel_id=1, source_target_pairs={{0,16},{8,24},{16,0},{24,8},{1,17},{9,25},{17,1},{25,9},{2,18},{10... | collective-permute-start | bytes 3145736 | tf_op jit(solution)/shard_map/ppermute | solution.py:56
  494.5 70.2 %collective-permute-start.39 = (bf16[4,4,64,1024]{3,2,1,0:T(8,128)(2,1)}, bf16[4,4,64,1024]{3,2,1,0:T(8,128)(2,1)}, u32[]{:S(2)}, u32[]{:S(2)}) collective-permute-start(bf16[4,4,64,1024]{3,2,1,0:T(8,128)(2,1)} %fusion.73), channel_id=1, source_target_pairs={{0,1},{1,0},{2,3},{3,2},{4,5},{5,4},{6,7},{7,6},{8,9},{9,8},{10,11... | collective-permute-start | bytes 6291464 | tf_op jit(solution)/shard_map/ppermute | solution.py:56
  525.6 137.9 %reduce-scatter.11.cloned.1.call-start = ((), (), s32[]{:S(2)}) async-start(), calls=%async_computation.9 | async-start | bytes 2621440 | tf_op jit(solution)/shard_map/reduce_scatter | solution.py:123
  542.6 30.2 %collective-permute-start.30 = (bf16[512,2048]{1,0:T(8,128)(2,1)}, bf16[512,2048]{1,0:T(8,128)(2,1)}, u32[]{:S(2)}, u32[]{:S(2)}) collective-permute-start(bf16[512,2048]{1,0:T(8,128)(2,1)} %convolution_convert_fusion.1), channel_id=1, source_target_pairs={{0,8},{8,0},{16,24},{24,16},{1,9},{9,1},{17,25},{25,17},{2,10},{10... | collective-permute-start | bytes 6291464 | tf_op jit(solution)/shard_map/ppermute | solution.py:56
  542.6 27.1 %collective-permute-start.32 = (bf16[256,2048]{1,0:T(8,128)(2,1)S(1)}, bf16[256,2048]{1,0:T(8,128)(2,1)}, u32[]{:S(2)}, u32[]{:S(2)}) collective-permute-start(bf16[256,2048]{1,0:T(8,128)(2,1)S(1)} %fusion.97), channel_id=1, source_target_pairs={{0,16},{8,24},{16,0},{24,8},{1,17},{9,25},{17,1},{25,9},{2,18},{10... | collective-permute-start | bytes 3145736 | tf_op jit(solution)/shard_map/ppermute | solution.py:56
  582.6 83.5 %collective-permute-start.31 = (bf16[256,2048]{1,0:T(8,128)(2,1)}, bf16[256,2048]{1,0:T(8,128)(2,1)}, u32[]{:S(2)}, u32[]{:S(2)}) collective-permute-start(bf16[256,2048]{1,0:T(8,128)(2,1)} %slice.250), channel_id=1, source_target_pairs={{0,16},{8,24},{16,0},{24,8},{1,17},{9,25},{17,1},{25,9},{2,18},{10... | collective-permute-start | bytes 3145736 | tf_op jit(solution)/shard_map/ppermute | solution.py:56
  644.0 94.0 %collective-permute-start.34 = (bf16[512,2048]{1,0:T(8,128)(2,1)}, bf16[512,2048]{1,0:T(8,128)(2,1)}, u32[]{:S(2)}, u32[]{:S(2)}) collective-permute-start(bf16[512,2048]{1,0:T(8,128)(2,1)} %convolution_convert_fusion), channel_id=1, source_target_pairs={{0,8},{8,0},{16,24},{24,16},{1,9},{9,1},{17,25},{25,17},{2,10},{10... | collective-permute-start | bytes 6291464 | tf_op jit(solution)/shard_map/ppermute | solution.py:56
  649.2 26.3 %collective-permute-start.46 = (bf16[1,4,64,2048]{3,2,1,0:T(8,128)(2,1)}, bf16[1,4,64,2048]{3,2,1,0:T(8,128)(2,1)}, u32[]{:S(2)}, u32[]{:S(2)}) collective-permute-start(bf16[1,4,64,2048]{3,2,1,0:T(8,128)(2,1)} %fusion.99), channel_id=1, source_target_pairs={{0,1},{1,0},{2,3},{3,2},{4,5},{5,4},{6,7},{7,6},{8,9},{9,8},{10,11... | collective-permute-start | bytes 3145736 | tf_op jit(solution)/shard_map/ppermute | solution.py:56
  659.1 49.7 %collective-permute-start.40 = (bf16[4,4,64,768]{3,2,1,0:T(8,128)(2,1)}, bf16[4,4,64,768]{3,2,1,0:T(8,128)(2,1)}, u32[]{:S(2)}, u32[]{:S(2)}) collective-permute-start(bf16[4,4,64,768]{3,2,1,0:T(8,128)(2,1)} %fusion.96), channel_id=1, source_target_pairs={{0,1},{1,0},{2,3},{3,2},{4,5},{5,4},{6,7},{7,6},{8,9},{9,8},{10,11... | collective-permute-start | bytes 4718600 | tf_op jit(solution)/shard_map/ppermute | solution.py:56
  677.3 36.7 %collective-permute-start.47 = (bf16[1,2,64,2048]{3,2,1,0:T(8,128)(2,1)S(1)}, bf16[1,2,64,2048]{3,2,1,0:T(8,128)(2,1)S(1)}, u32[]{:S(2)}, u32[]{:S(2)}) collective-permute-start(bf16[1,2,64,2048]{3,2,1,0:T(8,128)(2,1)S(1)} %fusion.108), channel_id=1, source_target_pairs={{0,2},{1,3},{2,0},{3,1},{4,6},{5,7},{6,4},{7,5},{8,10},{9,11},{10,... | collective-permute-start | bytes 1572872 | tf_op jit(solution)/shard_map/ppermute | solution.py:56
  711.6 24.8 %collective-permute-start.41 = (bf16[4,2,64,768]{3,2,1,0:T(8,128)(2,1)S(1)}, bf16[4,2,64,768]{3,2,1,0:T(8,128)(2,1)S(1)}, u32[]{:S(2)}, u32[]{:S(2)}) collective-permute-start(bf16[4,2,64,768]{3,2,1,0:T(8,128)(2,1)S(1)} %fusion.101), channel_id=1, source_target_pairs={{0,2},{1,3},{2,0},{3,1},{4,6},{5,7},{6,4},{7,5},{8,10},{9,11},{10,... | collective-permute-start | bytes 2359304 | tf_op jit(solution)/shard_map/ppermute | solution.py:56
  714.1 44.5 %collective-permute-start.48 = (bf16[1,1,64,2048]{3,2,1,0:T(8,128)(2,1)S(1)}, bf16[1,1,64,2048]{3,2,1,0:T(8,128)(2,1)S(1)}, u32[]{:S(2)}, u32[]{:S(2)}) collective-permute-start(bf16[1,1,64,2048]{3,2,1,0:T(8,128)(2,1)S(1)} %dynamic-slice_convert_fusion.5), channel_id=1, source_target_pairs={{0,4},{1,5},{2,6},{3,7},{4,0},{5,1},{6,2},{7,3},{8,12},{9,13},{10,... | collective-permute-start | bytes 786440 | tf_op jit(solution)/shard_map/ppermute | solution.py:56
  736.6 19.2 %collective-permute-start.42 = (bf16[4,1,64,768]{3,2,1,0:T(8,128)(2,1)S(1)}, bf16[4,1,64,768]{3,2,1,0:T(8,128)(2,1)S(1)}, u32[]{:S(2)}, u32[]{:S(2)}) collective-permute-start(bf16[4,1,64,768]{3,2,1,0:T(8,128)(2,1)S(1)} %dynamic-slice_convert_fusion.4), channel_id=1, source_target_pairs={{0,4},{1,5},{2,6},{3,7},{4,0},{5,1},{6,2},{7,3},{8,12},{9,13},{10,... | collective-permute-start | bytes 1179656 | tf_op jit(solution)/shard_map/ppermute | solution.py:56
  744.6 46.7 %collective-permute-start.35 = (bf16[256,2048]{1,0:T(8,128)(2,1)}, bf16[256,2048]{1,0:T(8,128)(2,1)S(1)}, u32[]{:S(2)}, u32[]{:S(2)}) collective-permute-start(bf16[256,2048]{1,0:T(8,128)(2,1)} %slice.249), channel_id=1, source_target_pairs={{0,16},{8,24},{16,0},{24,8},{1,17},{9,25},{17,1},{25,9},{2,18},{10... | collective-permute-start | bytes 3145736 | tf_op jit(solution)/shard_map/ppermute | solution.py:56
  757.2 19.6 %collective-permute-start.44 = (f32[64,768]{1,0:T(8,128)}, f32[64,768]{1,0:T(8,128)}, u32[]{:S(2)}, u32[]{:S(2)}) collective-permute-start(f32[64,768]{1,0:T(8,128)} %get-tuple-element.376), channel_id=1, source_target_pairs={{0,16},{8,24},{16,0},{24,8},{1,17},{9,25},{17,1},{25,9},{2,18},{10... | collective-permute-start | bytes 589832 | tf_op jit(solution)/shard_map/ppermute | solution.py:56
  797.4 26.5 %collective-permute-start.64 = (bf16[64,1024]{1,0:T(8,128)(2,1)}, bf16[64,1024]{1,0:T(8,128)(2,1)}, u32[]{:S(2)}, u32[]{:S(2)}) collective-permute-start(bf16[64,1024]{1,0:T(8,128)(2,1)} %get-tuple-element.384), channel_id=1, source_target_pairs={{0,8},{8,0},{16,24},{24,16},{1,9},{9,1},{17,25},{25,17},{2,10},{10... | collective-permute-start | bytes 393224 | tf_op jit(solution)/shard_map/ppermute | solution.py:56
  797.5 39.7 %collective-permute-start.65 = (bf16[64,1024]{1,0:T(8,128)(2,1)}, bf16[64,1024]{1,0:T(8,128)(2,1)}, u32[]{:S(2)}, u32[]{:S(2)}) collective-permute-start(bf16[64,1024]{1,0:T(8,128)(2,1)} %get-tuple-element.380), channel_id=1, source_target_pairs={{0,8},{8,0},{16,24},{24,16},{1,9},{9,1},{17,25},{25,17},{2,10},{10... | collective-permute-start | bytes 393224 | tf_op jit(solution)/shard_map/ppermute | solution.py:56
  798.0 39.2 %collective-permute-start.66 = (bf16[64,1024]{1,0:T(8,128)(2,1)}, bf16[64,1024]{1,0:T(8,128)(2,1)}, u32[]{:S(2)}, u32[]{:S(2)}) collective-permute-start(bf16[64,1024]{1,0:T(8,128)(2,1)} %get-tuple-element.383), channel_id=1, source_target_pairs={{0,16},{8,24},{16,0},{24,8},{1,17},{9,25},{17,1},{25,9},{2,18},{10... | collective-permute-start | bytes 393224 | tf_op jit(solution)/shard_map/ppermute | solution.py:56
  799.5 37.7 %collective-permute-start.67 = (bf16[64,1024]{1,0:T(8,128)(2,1)}, bf16[64,1024]{1,0:T(8,128)(2,1)}, u32[]{:S(2)}, u32[]{:S(2)}) collective-permute-start(bf16[64,1024]{1,0:T(8,128)(2,1)} %get-tuple-element.379), channel_id=1, source_target_pairs={{0,16},{8,24},{16,0},{24,8},{1,17},{9,25},{17,1},{25,9},{2,18},{10... | collective-permute-start | bytes 393224 | tf_op jit(solution)/shard_map/ppermute | solution.py:56
  (137 other events, 1932.5 us)
Sparse Core Ops, SparseCore 0:
  28.7 62.3 all-gather.2
  137.8 201.2 all-gather.4
  420.3 43.6 reduce-scatter.4
  466.7 42.8 reduce-scatter.6
  525.7 43.6 reduce-scatter.8
  572.1 42.8 reduce-scatter.10
